TPU v7x, 32 devices: a whole 2x2x4 slice. The times are simulated.
32 devices in a mesh: rep: 2 (over y), ep: 8 (over z, x), tp: 2 (over core).
Axes of the slice: x: 2, y: 2, z: 4, core: 2. Of those that a mesh axis runs over, the one named last changes fastest.
Arguments:
- resid: bfloat16 [1024, 1440], P(('rep', 'ep')), parts along dimension 0, may hold values from -6 to 6
- query: bfloat16 [1024, 2048], P(('rep', 'ep'), 'tp'), parts along dimension 0, may hold values from -400 to 400
- key_value_pages: bfloat16 [2, 12288, 16, 256], P(None, ('rep', 'ep'), None, 'tp'), parts along dimension 1, may hold values from -4 to 4
- page_table: int32 [1024, 12], P(('rep', 'ep')), parts along dimension 0, may hold values from 0 to 767, as said below
- ctx_len: int32 [1024], P(('rep', 'ep')), parts along dimension 0, may hold values from 2 to 192, as said below
- experts_chosen: int32 [1024, 4], P(('rep', 'ep')), parts along dimension 0, may hold values from 0 to 7, as said below
- router_logits: float32 [1024, 4], P(('rep', 'ep')), parts along dimension 0, may hold values from -25 to 300
- norm_gain: float32 [1440], replicated, may hold values from 0.25 to 1.75
- out_proj: bfloat16 [2048, 1440], P('tp'), may hold values from -0.125 to 0.125
- w_gate: bfloat16 [8, 1440, 1440], P('ep', None, 'tp'), may hold values from -0.15625 to 0.15625
- w_up: bfloat16 [8, 1440, 1440], P('ep', None, 'tp'), may hold values from -0.15625 to 0.15625
- w_down: bfloat16 [8, 1440, 1440], P('ep', 'tp'), may hold values from -3 to 3
Outputs:
- mixed: bfloat16 [1024, 1440], P(('rep', 'ep'), 'tp'), parts along dimension 0
There are 2 independent parts, one for each index of `rep`. A program takes and returns all parts, laid end to end along the dimension named above; an argument that names none is the same for every part. Nothing has to cross between parts.
Inputs may be any that keep to these rules, and one draw needn't show every extreme that they name: Each block of 64 tokens holds its own pool: the rows of page_table of one block together name each of its 768 pages once. `ctx_len`: every block of 64 tokens has a token with 192 positions. `experts_chosen`: each row names 4 different experts. Within the rows of one device no expert is named by more than 64 rows, and one expert is named by exactly 64 of them.
All inputs are finite; a program needn't handle non-finite values.
Results may differ from a plain program's by a relative error of at most 0.008.
Values may be sent and summed in bfloat16 or wider, within the bound.
No kernel may reach another device: no remote copies, remote signals or barrier semaphores. Data moves between devices by JAX's collectives and lax.ppermute only.
A program may use at most 128 MiB of HBM per device.

v0:
```python
import functools
import math

import jax
import jax.numpy as jnp
from jax import lax
from jax.experimental import pallas as pl
from jax.experimental.pallas import tpu as pltpu
from jax.sharding import PartitionSpec as P


HEAD_WIDTH = 64
LANES = 128
MIB = 1 << 20

SMEM = pl.BlockSpec(memory_space=pltpu.SMEM)
VMEM = pl.BlockSpec(memory_space=pltpu.VMEM)
HBM = pl.BlockSpec(memory_space=pltpu.HBM)


def dense_gates(experts, chosen, logits, out):
    tokens, columns = out.shape
    gate = jnp.exp(logits[...] - jnp.max(logits[...], axis=0, keepdims=True))
    gate = gate / jnp.sum(gate, axis=0, keepdims=True)
    name = lax.broadcasted_iota(jnp.int32, (columns, tokens), 0)
    fine = name >= experts
    expert = jnp.where(fine, name - experts, name)
    dense = jnp.zeros((columns, tokens), jnp.float32)
    for k in range(chosen.shape[0]):
        dense += jnp.where(chosen[k : k + 1, :] == expert, gate[k : k + 1, :], 0.0)
    coarse = dense.astype(jnp.bfloat16).astype(jnp.float32)
    both = jnp.where(fine, dense - coarse, coarse).astype(jnp.bfloat16)
    row = lax.broadcasted_iota(jnp.int32, (columns, columns), 0)
    unit = (row == lax.broadcasted_iota(jnp.int32, (columns, columns), 1)).astype(jnp.bfloat16)
    turned = lax.dot_general(both, unit, (((0,), (0,)), ((), ())), preferred_element_type=jnp.float32)
    out[...] = turned.astype(jnp.bfloat16)


def attend_kernel(
    heads,
    unroll,
    experts,
    table,
    length,
    q_ref,
    pages,
    proj,
    chosen,
    logits,
    out_wide,
    out_sent,
    out_gates,
    kbuf,
    vbuf,
    wbuf,
    qs,
    os,
    sem,
):
    tokens = q_ref.shape[0]
    per_token = table.shape[0]
    lanes = kbuf.shape[2]
    positions = per_token * kbuf.shape[1]
    copies = [
        pltpu.make_async_copy(pages.at[0], kbuf, sem.at[0]),
        pltpu.make_async_copy(pages.at[1], vbuf, sem.at[1]),
        pltpu.make_async_copy(proj, wbuf, sem.at[2]),
    ]
    for copy in copies:
        copy.start()
    low = lax.broadcasted_iota(jnp.int32, (tokens, lanes), 1) < HEAD_WIDTH
    half = heads // 2
    for h in range(heads):
        pair = q_ref[:, (h // 2) * lanes : (h // 2 + 1) * lanes].astype(jnp.float32)
        if (h < half) != (h % 2 == 0):
            pair = pltpu.roll(pair, HEAD_WIDTH, 1)
        row = jnp.where(low if h < half else ~low, pair, 0.0)
        qs[pl.ds(h, tokens, stride=heads), :] = row * (1.0 / math.sqrt(HEAD_WIDTH))
    dense_gates(experts, chosen, logits, out_gates)
    copies[0].wait()
    copies[1].wait()
    spot = lax.broadcasted_iota(jnp.int32, (heads, positions), 1)

    @pl.loop(0, tokens // unroll)
    def _(step):
        scores, values = [], []
        for u in range(unroll):
            t = step * unroll + u
            ids = [table[i, t] for i in range(per_token)]
            keys = jnp.concatenate([kbuf[i] for i in ids], axis=0)
            values.append(jnp.concatenate([vbuf[i] for i in ids], axis=0))
            q = qs[pl.ds(pl.multiple_of(t * heads, heads), heads), :].astype(jnp.bfloat16)
            s = lax.dot_general(
                q, keys, (((1,), (1,)), ((), ())), preferred_element_type=jnp.float32
            )
            scores.append(jnp.where(spot < length[t], s, -jnp.inf))
        s = jnp.concatenate(scores, axis=0)
        w = jnp.exp(s - jnp.max(s, axis=1, keepdims=True))
        total = jnp.sum(w, axis=1, keepdims=True)
        p = w.astype(jnp.bfloat16)
        o = jnp.concatenate(
            [
                jnp.dot(p[u * heads : (u + 1) * heads], values[u], preferred_element_type=jnp.float32)
                for u in range(unroll)
            ],
            axis=0,
        )
        rows = unroll * heads
        os[pl.ds(pl.multiple_of(step * rows, rows), rows), :] = o / total

    parts = []
    for j in range(half):
        even = os[pl.ds(2 * j, tokens, stride=heads), :]
        odd = os[pl.ds(2 * j + 1, tokens, stride=heads), :]
        if 2 * j < half:
            odd = pltpu.roll(odd, HEAD_WIDTH, 1)
        else:
            even = pltpu.roll(even, HEAD_WIDTH, 1)
        parts.append(jnp.where(low, even, odd).astype(jnp.bfloat16))
    attended = jnp.concatenate(parts, axis=1)
    copies[2].wait()
    part = lax.dot_general(
        attended, wbuf[...], (((1,), (1,)), ((), ())), preferred_element_type=jnp.float32
    )
    out_wide[...] = part
    out_sent[...] = part.astype(jnp.bfloat16)


def attend(query, pages, page_table, ctx_len, out_proj, chosen, logits, experts):
    tokens = query.shape[0]
    heads = query.shape[1] // HEAD_WIDTH
    width = out_proj.shape[1]
    lanes = pages.shape[3]
    rows = (tokens * heads, lanes)
    operands = (page_table.T, ctx_len, query, pages, out_proj.T, chosen.T, logits.T)
    operands = [pltpu.with_memory_space_constraint(v, pltpu.HBM) for v in operands]
    return pl.pallas_call(
        functools.partial(attend_kernel, heads, min(16, tokens), experts),
        out_shape=(
            jax.ShapeDtypeStruct((tokens, width), jnp.float32),
            jax.ShapeDtypeStruct((tokens, width), jnp.bfloat16),
            jax.ShapeDtypeStruct((tokens, 2 * experts), jnp.bfloat16),
        ),
        in_specs=[SMEM, SMEM, VMEM, HBM, HBM, VMEM, VMEM],
        out_specs=(VMEM,) * 3,
        scratch_shapes=[
            pltpu.VMEM(pages.shape[1:], pages.dtype),
            pltpu.VMEM(pages.shape[1:], pages.dtype),
            pltpu.VMEM(out_proj.shape[::-1], out_proj.dtype),
            pltpu.VMEM(rows, jnp.float32),
            pltpu.VMEM(rows, jnp.float32),
            pltpu.SemaphoreType.DMA((3,)),
        ],
        compiler_params=pltpu.CompilerParams(vmem_limit_bytes=50 * MIB),
        name="attend",
    )(*operands)


def norm_kernel(resid, own, other, gain, gates, stream_out, all_out, mine_out):
    tokens, width = own.shape
    side = lax.axis_index("tp")
    half_cols = stream_out.shape[1]
    stream = resid[...].astype(jnp.float32) + own[...] + other[...].astype(jnp.float32)
    mean_square = jnp.sum(stream * stream, axis=1, keepdims=True) / width
    normed = stream * lax.rsqrt(mean_square + 1e-05) * gain[...]
    all_out[:, :width] = normed.astype(jnp.bfloat16)
    all_out[:, width : width + gates.shape[1]] = gates[...]
    rows = tokens // 2
    mine_out[...] = all_out[pl.ds(pl.multiple_of(side * rows, rows), rows), :]
    stream_out[...] = jnp.where(side == 0, stream[:, :half_cols], stream[:, half_cols:])


def norm(resid, own, other, gain, gates, padded):
    tokens, width = own.shape
    return pl.pallas_call(
        norm_kernel,
        out_shape=(
            jax.ShapeDtypeStruct((tokens, width // 2), jnp.float32),
            jax.ShapeDtypeStruct((tokens, padded), jnp.bfloat16),
            jax.ShapeDtypeStruct((tokens // 2, padded), jnp.bfloat16),
        ),
        in_specs=[VMEM] * 5,
        out_specs=(VMEM,) * 3,
        compiler_params=pltpu.CompilerParams(vmem_limit_bytes=4 * MIB),
        name="norm",
    )(resid, own, other, gain[None], gates)


def expert_kernel(experts, pieces, *refs):
    sources = refs[:pieces]
    w_gate, w_up, w_down, keep_out, send_out, xs = refs[pieces:]
    side = lax.axis_index("tp")
    me = lax.axis_index("ep")
    width = w_gate.shape[0]
    if pieces == 1:
        xs = sources[0]
    else:
        rows = sources[0].shape[0]
        for b in range(pieces // 2):
            here = pl.multiple_of(b * 2 * rows + side * rows, rows)
            there = pl.multiple_of(b * 2 * rows + (1 - side) * rows, rows)
            xs[pl.ds(here, rows), :] = sources[2 * b][...]
            xs[pl.ds(there, rows), :] = sources[2 * b + 1][...]
    x = xs[:, :width]
    spare = xs[:, width : width + 2 * experts].astype(jnp.float32)
    column = lax.broadcasted_iota(jnp.int32, spare.shape, 1)
    mine = (column == me) | (column == me + experts)
    gate = jnp.sum(jnp.where(mine, spare, 0.0), axis=1, keepdims=True)
    g = jnp.dot(x, w_gate[...], preferred_element_type=jnp.float32)
    u = jnp.dot(x, w_up[...], preferred_element_type=jnp.float32)
    hidden = (g * jax.nn.sigmoid(1.702 * g) * (u + 1.0)).astype(jnp.bfloat16)
    y = jnp.dot(hidden, w_down[...], preferred_element_type=jnp.float32) * gate
    half_cols = y.shape[1] // 2
    left, right = y[:, :half_cols], y[:, half_cols:]
    keep_out[:, :half_cols] = jnp.where(side == 0, left, right)
    send_out[:, :half_cols] = jnp.where(side == 0, right, left).astype(jnp.bfloat16)


def expert(sources, w_gate, w_up, w_down, experts):
    pieces = len(sources)
    rows = sum(s.shape[0] for s in sources)
    padded = sources[0].shape[1]
    out_cols = -(-w_down.shape[1] // 2 // LANES) * LANES
    return pl.pallas_call(
        functools.partial(expert_kernel, experts, pieces),
        out_shape=(
            jax.ShapeDtypeStruct((rows, out_cols), jnp.float32),
            jax.ShapeDtypeStruct((rows, out_cols), jnp.bfloat16),
        ),
        in_specs=[VMEM] * (pieces + 3),
        out_specs=(VMEM,) * 2,
        scratch_shapes=[pltpu.VMEM((rows if pieces > 1 else 16, padded), jnp.bfloat16)],
        compiler_params=pltpu.CompilerParams(vmem_limit_bytes=16 * MIB),
        cost_estimate=pl.CostEstimate(
            flops=6 * rows * w_down.size, transcendentals=0, bytes_accessed=6 * w_down.size
        ),
        name="expert",
    )(*sources, w_gate, w_up, w_down)


def flip(value, axis, offset):
    return lax.ppermute(value, axis, [(i, i ^ offset) for i in range(lax.axis_size(axis))])


def step_from(k, owners):
    return 0 if k == owners - 1 else k & (k - 1)


def routed_all(stream, whole, mine, w_gate, w_up, w_down, experts):
    owners = lax.axis_size("ep")
    tokens = whole.shape[0]
    near = [k for k in range(1, owners) if k & (k - 1) == 0]
    far = [k for k in range(1, owners) if k not in near]
    half = {0: mine}
    for k in sorted(near, reverse=True) + sorted(far, key=lambda k: (k.bit_count(), -k)):
        source = step_from(k, owners)
        half[k] = flip(half[source], "ep", k ^ source)
    total = {}
    for name, group in (("own", [0]), ("near", near), ("far", far)):
        sources = [whole]
        if name != "own":
            sources = []
            for k in group:
                sources += [half[k], flip(half[k], "tp", 1)]
        kept, sent = expert(sources, w_gate[0], w_up[0], w_down[0], experts)
        received = flip(sent, "tp", 1)
        for i, k in enumerate(group):
            rows = slice(i * tokens, (i + 1) * tokens)
            total[k] = kept[rows] + received[rows].astype(jnp.float32)
    for k in sorted(range(1, owners), key=lambda k: (-k.bit_count(), -k)):
        target = step_from(k, owners)
        part = flip(total[k].astype(jnp.bfloat16), "ep", k ^ target)
        total[target] = total[target] + part.astype(jnp.float32)
    return (stream + total[0][:, : stream.shape[1]]).astype(jnp.bfloat16)


def routed_slots(stream, normed, experts_chosen, router_logits, w_gate, w_up, w_down, capacity):
    tok_rows, top_count = experts_chosen.shape
    local_experts = w_gate.shape[0]
    owners = lax.axis_size("ep")
    experts = local_experts * owners
    gate_weights = jax.nn.softmax(router_logits, axis=1)
    chosen_flat = experts_chosen.reshape(-1)
    onehot = (chosen_flat[:, None] == jnp.arange(experts, dtype=jnp.int32)[None, :]).astype(
        jnp.int32
    )
    before = jnp.cumsum(onehot, axis=0, dtype=jnp.int32) - onehot
    slot_rank = jnp.sum(before * onehot, axis=1, dtype=jnp.int32)
    slot_index = (chosen_flat * capacity + slot_rank).reshape(tok_rows, top_count)
    slot_range = jnp.arange(experts * capacity, dtype=jnp.int32)
    placed = slot_index[:, :, None] == slot_range[None, None, :]
    dispatch = jnp.sum(placed.astype(jnp.float32), axis=1).astype(jnp.bfloat16)
    outgoing = lax.dot_general(
        dispatch, normed, (((0,), (0,)), ((), ())), preferred_element_type=jnp.float32
    )
    outgoing = outgoing.astype(jnp.bfloat16).reshape(
        owners, local_experts, capacity, normed.shape[1]
    )
    arrived_full = lax.all_gather(
        lax.all_to_all(outgoing, "ep", split_axis=0, concat_axis=0, tiled=True),
        "tp",
        axis=3,
        tiled=True,
    )
    gate_value = jnp.einsum(
        "sekd,edf->sekf", arrived_full, w_gate, preferred_element_type=jnp.float32
    )
    up_value = jnp.einsum("sekd,edf->sekf", arrived_full, w_up, preferred_element_type=jnp.float32)
    hidden = (gate_value * jax.nn.sigmoid(1.702 * gate_value) * (up_value + 1.0)).astype(
        jnp.bfloat16
    )
    partial_value = jnp.einsum("sekf,efd->sekd", hidden, w_down, preferred_element_type=jnp.float32)
    finished = lax.psum_scatter(partial_value, "tp", scatter_dimension=3, tiled=True).astype(
        jnp.bfloat16
    )
    returned = lax.all_to_all(finished, "ep", split_axis=0, concat_axis=0, tiled=True)
    combine = jnp.sum(placed.astype(jnp.float32) * gate_weights[:, :, None], axis=1)
    expert_mix = jnp.dot(
        combine,
        returned.reshape(experts * capacity, -1).astype(jnp.float32),
        precision=lax.Precision.HIGHEST,
    )
    return (stream + expert_mix).astype(jnp.bfloat16)


def layer(
    resid,
    query,
    key_value_pages,
    page_table,
    ctx_len,
    experts_chosen,
    router_logits,
    norm_gain,
    out_proj,
    w_gate,
    w_up,
    w_down,
):
    tok_rows, model_width = resid.shape
    top_count = experts_chosen.shape[1]
    local_experts = w_gate.shape[0]
    owners = lax.axis_size("ep")
    experts = local_experts * owners
    capacity = max(2, min(tok_rows, 2 * tok_rows * top_count // experts))
    padded = -(-model_width // LANES) * LANES

    own, sent, gates = attend(
        query, key_value_pages, page_table, ctx_len, out_proj, experts_chosen, router_logits, experts
    )
    other = flip(sent, "tp", 1)
    if (
        local_experts == 1
        and tok_rows <= capacity
        and model_width + 2 * experts <= padded
        and owners & (owners - 1) == 0
    ):
        stream, whole, mine = norm(resid, own, other, norm_gain, gates, padded)
        return routed_all(stream, whole, mine, w_gate, w_up, w_down, experts)
    half_cols = model_width // lax.axis_size("tp")
    offset = lax.axis_index("tp") * half_cols
    stream = resid.astype(jnp.float32) + own + other.astype(jnp.float32)
    mean_square = jnp.mean(stream * stream, axis=1, keepdims=True)
    normed = (stream * lax.rsqrt(mean_square + 1e-05) * norm_gain).astype(jnp.bfloat16)
    stream = lax.dynamic_slice_in_dim(stream, offset, half_cols, 1)
    normed = lax.dynamic_slice_in_dim(normed, offset, half_cols, 1)
    return routed_slots(
        stream, normed, experts_chosen, router_logits, w_gate, w_up, w_down, capacity
    )


def solution(mesh):
    return jax.shard_map(
        layer,
        mesh=mesh,
        in_specs=(
            P(("rep", "ep"), None),
            P(("rep", "ep"), "tp"),
            P(None, ("rep", "ep"), None, "tp"),
            P(("rep", "ep"), None),
            P(("rep", "ep")),
            P(("rep", "ep"), None),
            P(("rep", "ep"), None),
            P(),
            P("tp", None),
            P("ep", None, "tp"),
            P("ep", None, "tp"),
            P("ep", "tp", None),
        ),
        out_specs=P(("rep", "ep"), "tp"),
        check_vma=False,
    )
```

profile of v0, /device:TPU:0, one launch (start us, length us, event | category | flops | bytes accessed | tf_op | source)
XLA Modules:
  0.0 58.3 jit_solution(2925326921834635244)
XLA Ops:
  0.0 8.8 %attend.1 = (f32[64,1440]{1,0:T(8,128)S(1)}, bf16[64,1440]{1,0:T(8,128)(2,1)S(1)}, bf16[64,16]{1,0:T(8,128)(2,1)S(1)}) custom-call(s32[12,64]{1,0:T(8,128)} %bitcast.17, s32[64]{0:T(128)} %length.1, bf16[64,1024]{1,0:T(8,128)(2,1)} %q_ref.1, bf16[2,768,16,128]{3,2,1,0:T(8,128)(2,1)} %pages.1, bf16[1440,1024]{1,0:T(8,128)(2,1)} %bitcast.16, ...), custom_call_target="tpu_custom_call" | custom-call | tf_op jit(solution)/shard_map/attend/pallas_call | solution.py:137
  8.8 0.6 collective-permute-start
  9.4 1.1 %collective-permute-done.other = bf16[64,1440]{1,0:T(8,128)(2,1)S(1)} collective-permute-done((bf16[64,1440]{1,0:T(8,128)(2,1)S(1)}, bf16[64,1440]{1,0:T(8,128)(2,1)S(1)}, u32[]{:S(2)}, u32[]{:S(2)}) %collective-permute-start) | collective-permute-done | bytes 184352 | tf_op jit(solution)/shard_map/ppermute | solution.py:242
  10.5 0.2 norm.1
  10.7 4.0 %collective-permute-start.5 = (bf16[32,1536]{1,0:T(8,128)(2,1)S(1)}, bf16[32,1536]{1,0:T(8,128)(2,1)S(1)}, u32[]{:S(2)}, u32[]{:S(2)}) collective-permute-start(bf16[32,1536]{1,0:T(8,128)(2,1)S(1)} %get-tuple-element.24), channel_id=1, source_target_pairs={{0,8},{2,10},{4,12},{6,14},{8,0},{10,2},{12,4},{14,6},{1,9},{3,11}... | collective-permute-start | bytes 294920 | tf_op jit(solution)/shard_map/ppermute | solution.py:242
  14.7 1.6 %collective-permute-start.2 = (bf16[32,1536]{1,0:T(8,128)(2,1)S(1)}, bf16[32,1536]{1,0:T(8,128)(2,1)S(1)}, u32[]{:S(2)}, u32[]{:S(2)}) collective-permute-start(bf16[32,1536]{1,0:T(8,128)(2,1)S(1)} %get-tuple-element.24), channel_id=1, source_target_pairs={{0,4},{2,6},{4,0},{6,2},{8,12},{10,14},{12,8},{14,10},{1,5},{3,7},... | collective-permute-start | bytes 294920 | tf_op jit(solution)/shard_map/ppermute | solution.py:242
  16.3 1.1 %collective-permute-start.10 = (bf16[32,1536]{1,0:T(8,128)(2,1)S(1)}, bf16[32,1536]{1,0:T(8,128)(2,1)S(1)}, u32[]{:S(2)}, u32[]{:S(2)}) collective-permute-start(bf16[32,1536]{1,0:T(8,128)(2,1)S(1)} %get-tuple-element.24), channel_id=1, source_target_pairs={{0,14},{2,12},{4,10},{6,8},{8,6},{10,4},{12,2},{14,0},{1,15},{3,13... | collective-permute-start | bytes 294920 | tf_op jit(solution)/shard_map/ppermute | solution.py:242
  17.4 2.9 %collective-permute-done.5.refs_4_ = bf16[32,1536]{1,0:T(8,128)(2,1)S(1)} collective-permute-done((bf16[32,1536]{1,0:T(8,128)(2,1)S(1)}, bf16[32,1536]{1,0:T(8,128)(2,1)S(1)}, u32[]{:S(2)}, u32[]{:S(2)}) %collective-permute-start.5) | collective-permute-done | bytes 98336 | tf_op jit(solution)/shard_map/ppermute | solution.py:242
  20.3 2.5 %collective-permute-start.6 = (bf16[32,1536]{1,0:T(8,128)(2,1)S(1)}, bf16[32,1536]{1,0:T(8,128)(2,1)S(1)}, u32[]{:S(2)}, u32[]{:S(2)}) collective-permute-start(bf16[32,1536]{1,0:T(8,128)(2,1)S(1)} %collective-permute-done.5.refs_4_), channel_id=1, source_target_pairs={{0,2},{2,0},{4,6},{6,4},{8,10},{10,8},{12,14},{14,12},{1,3},{3,1},... | collective-permute-start | bytes 294920 | tf_op jit(solution)/shard_map/ppermute | solution.py:242
  22.9 0.0 collective-permute-start.8
  22.9 0.0 collective-permute-done.2.refs_2_
  22.9 0.5 collective-permute-start.3
  23.3 0.9 %collective-permute-done.10.refs_6_ = bf16[32,1536]{1,0:T(8,128)(2,1)S(1)} collective-permute-done((bf16[32,1536]{1,0:T(8,128)(2,1)S(1)}, bf16[32,1536]{1,0:T(8,128)(2,1)S(1)}, u32[]{:S(2)}, u32[]{:S(2)}) %collective-permute-start.10) | collective-permute-done | bytes 98336 | tf_op jit(solution)/shard_map/ppermute | solution.py:242
  24.3 0.0 collective-permute-start.11
  24.3 2.2 %collective-permute-done.6.refs_2_ = bf16[32,1536]{1,0:T(8,128)(2,1)S(1)} collective-permute-done((bf16[32,1536]{1,0:T(8,128)(2,1)S(1)}, bf16[32,1536]{1,0:T(8,128)(2,1)S(1)}, u32[]{:S(2)}, u32[]{:S(2)}) %collective-permute-start.6) | collective-permute-done | bytes 98336 | tf_op jit(solution)/shard_map/ppermute | solution.py:242
  26.5 0.0 collective-permute-start.7
  26.5 1.0 %collective-permute-done.8.refs_4_ = bf16[32,1536]{1,0:T(8,128)(2,1)S(1)} collective-permute-done((bf16[32,1536]{1,0:T(8,128)(2,1)S(1)}, bf16[32,1536]{1,0:T(8,128)(2,1)S(1)}, u32[]{:S(2)}, u32[]{:S(2)}) %collective-permute-start.8) | collective-permute-done | bytes 98336 | tf_op jit(solution)/shard_map/ppermute | solution.py:242
  27.5 0.0 collective-permute-start.9
  27.5 0.3 collective-permute-done.3.refs_0_
  27.7 0.2 collective-permute-start.4
  28.0 0.0 collective-permute-done.11.refs_7_
  28.0 0.8 %collective-permute-done.9.refs_5_ = bf16[32,1536]{1,0:T(8,128)(2,1)S(1)} collective-permute-done((bf16[32,1536]{1,0:T(8,128)(2,1)S(1)}, bf16[32,1536]{1,0:T(8,128)(2,1)S(1)}, u32[]{:S(2)}, u32[]{:S(2)}) %collective-permute-start.9) | collective-permute-done | bytes 98336 | tf_op jit(solution)/shard_map/ppermute | solution.py:242
  28.8 0.3 collective-permute-done.4.refs_1_
  29.1 2.3 %expert.4 = (f32[256,768]{1,0:T(8,128)S(1)}, bf16[256,768]{1,0:T(8,128)(2,1)S(1)}) custom-call(bf16[32,1536]{1,0:T(8,128)(2,1)S(1)} %collective-permute-done.3.refs_0_, bf16[32,1536]{1,0:T(8,128)(2,1)S(1)} %collective-permute-done.4.refs_1_, bf16[32,1536]{1,0:T(8,128)(2,1)S(1)} %collective-permute-done.6.refs_2_, ...), custom_call_target="tpu_custom_call" | custom-call | flops 1592524800 | bytes 6220800 | tf_op jit(solution)/shard_map/expert/pallas_call | solution.py:224
  31.4 0.3 collective-permute-start.12
  31.7 1.2 %collective-permute-start.14 = (bf16[32,1536]{1,0:T(8,128)(2,1)S(1)}, bf16[32,1536]{1,0:T(8,128)(2,1)S(1)}, u32[]{:S(2)}, u32[]{:S(2)}) collective-permute-start(bf16[32,1536]{1,0:T(8,128)(2,1)S(1)} %get-tuple-element.24), channel_id=1, source_target_pairs={{0,2},{2,0},{4,6},{6,4},{8,10},{10,8},{12,14},{14,12},{1,3},{3,1},... | collective-permute-start | bytes 294920 | tf_op jit(solution)/shard_map/ppermute | solution.py:242
  32.9 0.1 collective-permute-start.17
  33.0 0.4 collective-permute-start.16
  33.4 3.3 %collective-permute-done.14.refs_0_ = bf16[32,1536]{1,0:T(8,128)(2,1)S(1)} collective-permute-done((bf16[32,1536]{1,0:T(8,128)(2,1)S(1)}, bf16[32,1536]{1,0:T(8,128)(2,1)S(1)}, u32[]{:S(2)}, u32[]{:S(2)}) %collective-permute-start.14) | collective-permute-done | bytes 98336 | tf_op jit(solution)/shard_map/ppermute | solution.py:242
  36.7 1.3 %collective-permute-done.15.refs_1_ = bf16[32,1536]{1,0:T(8,128)(2,1)S(1)} collective-permute-done((bf16[32,1536]{1,0:T(8,128)(2,1)S(1)}, bf16[32,1536]{1,0:T(8,128)(2,1)S(1)}, u32[]{:S(2)}, u32[]{:S(2)}) %collective-permute-start.15) | collective-permute-done | bytes 98336 | tf_op jit(solution)/shard_map/ppermute | solution.py:242
  37.9 1.8 %expert.5 = (f32[192,768]{1,0:T(8,128)S(1)}, bf16[192,768]{1,0:T(8,128)(2,1)S(1)}) custom-call(bf16[32,1536]{1,0:T(8,128)(2,1)S(1)} %collective-permute-done.14.refs_0_, bf16[32,1536]{1,0:T(8,128)(2,1)S(1)} %collective-permute-done.15.refs_1_, bf16[32,1536]{1,0:T(8,128)(2,1)S(1)} %collective-permute-done.2.refs_2_, ...), custom_call_target="tpu_custom_call" | custom-call | flops 1194393600 | bytes 6220800 | tf_op jit(solution)/shard_map/expert/pallas_call | solution.py:224
  39.8 0.2 collective-permute-start.18
  40.0 0.1 add_convert_fusion.6
  40.1 1.8 %collective-permute-start.19 = (bf16[64,768]{1,0:T(8,128)(2,1)S(1)}, bf16[64,768]{1,0:T(8,128)(2,1)S(1)}, u32[]{:S(2)}, u32[]{:S(2)}) collective-permute-start(bf16[64,768]{1,0:T(8,128)(2,1)S(1)} %get-tuple-element.32), channel_id=1, source_target_pairs={{0,4},{2,6},{4,0},{6,2},{8,12},{10,14},{12,8},{14,10},{1,5},{3,7},... | collective-permute-start | bytes 294920 | tf_op jit(solution)/shard_map/ppermute | solution.py:242
  41.9 0.3 collective-permute-start.20
  42.2 1.7 %collective-permute-start.22 = (bf16[64,768]{1,0:T(8,128)(2,1)S(1)}, bf16[64,768]{1,0:T(8,128)(2,1)S(1)}, u32[]{:S(2)}, u32[]{:S(2)}) collective-permute-start(bf16[64,768]{1,0:T(8,128)(2,1)S(1)} %get-tuple-element.30), channel_id=1, source_target_pairs={{0,2},{2,0},{4,6},{6,4},{8,10},{10,8},{12,14},{14,12},{1,3},{3,1},... | collective-permute-start | bytes 294920 | tf_op jit(solution)/shard_map/ppermute | solution.py:242
  43.9 1.4 %expert.3 = (f32[64,768]{1,0:T(8,128)S(1)}, bf16[64,768]{1,0:T(8,128)(2,1)S(1)}) custom-call(bf16[64,1536]{1,0:T(8,128)(2,1)S(1)} %get-tuple-element.21.refs_0_, bf16[1440,720]{1,0:T(8,128)(2,1)S(1)} %bitcast.9, bf16[1440,720]{1,0:T(8,128)(2,1)S(1)} %bitcast.12, bf16[720,1440]{1,0:T(8,128)(2,1)S(1)} %bitcast.15), custom_call_target="tpu_custom_call" | custom-call | flops 398131200 | bytes 6220800 | tf_op jit(solution)/shard_map/expert/pallas_call | solution.py:224
  45.4 0.1 collective-permute-start.1
  45.5 3.0 %collective-permute-start.13 = (bf16[64,768]{1,0:T(8,128)(2,1)S(1)}, bf16[64,768]{1,0:T(8,128)(2,1)S(1)}, u32[]{:S(2)}, u32[]{:S(2)}) collective-permute-start(bf16[64,768]{1,0:T(8,128)(2,1)S(1)} %get-tuple-element.29), channel_id=1, source_target_pairs={{0,14},{2,12},{4,10},{6,8},{8,6},{10,4},{12,2},{14,0},{1,15},{3,13... | collective-permute-start | bytes 294920 | tf_op jit(solution)/shard_map/ppermute | solution.py:242
  48.5 0.3 collective-permute-done.22
  48.8 0.1 add_convert_fusion.3
  48.9 2.2 %collective-permute-start.21 = (bf16[64,768]{1,0:T(8,128)(2,1)S(1)}, bf16[64,768]{1,0:T(8,128)(2,1)S(1)}, u32[]{:S(2)}, u32[]{:S(2)}) collective-permute-start(bf16[64,768]{1,0:T(8,128)(2,1)S(1)} %get-tuple-element.33), channel_id=1, source_target_pairs={{0,8},{2,10},{4,12},{6,14},{8,0},{10,2},{12,4},{14,6},{1,9},{3,11}... | collective-permute-start | bytes 294920 | tf_op jit(solution)/shard_map/ppermute | solution.py:242
  51.1 1.4 %collective-permute-start.23 = (bf16[64,768]{1,0:T(8,128)(2,1)S(1)}, bf16[64,768]{1,0:T(8,128)(2,1)S(1)}, u32[]{:S(2)}, u32[]{:S(2)}) collective-permute-start(bf16[64,768]{1,0:T(8,128)(2,1)S(1)} %get-tuple-element.35), channel_id=1, source_target_pairs={{0,4},{2,6},{4,0},{6,2},{8,12},{10,14},{12,8},{14,10},{1,5},{3,7},... | collective-permute-start | bytes 294920 | tf_op jit(solution)/shard_map/ppermute | solution.py:242
  52.5 0.5 collective-permute-start.24
  53.0 1.0 %collective-permute-done.13 = bf16[64,768]{1,0:T(8,128)(2,1)S(1)} collective-permute-done((bf16[64,768]{1,0:T(8,128)(2,1)S(1)}, bf16[64,768]{1,0:T(8,128)(2,1)S(1)}, u32[]{:S(2)}, u32[]{:S(2)}) %collective-permute-start.13) | collective-permute-done | bytes 98336 | tf_op jit(solution)/shard_map/ppermute | solution.py:242
  54.0 3.5 %collective-permute-done.21 = bf16[64,768]{1,0:T(8,128)(2,1)S(1)} collective-permute-done((bf16[64,768]{1,0:T(8,128)(2,1)S(1)}, bf16[64,768]{1,0:T(8,128)(2,1)S(1)}, u32[]{:S(2)}, u32[]{:S(2)}) %collective-permute-start.21) | collective-permute-done | bytes 98336 | tf_op jit(solution)/shard_map/ppermute | solution.py:242
  57.5 0.1 collective-permute-done.23
  57.6 0.7 %fusion.5 = bf16[64,720]{1,0:T(8,128)(2,1)} fusion(f32[64,720]{1,0:T(8,128)S(1)} %get-tuple-element.20, f32[64,768]{1,0:T(8,128)S(1)} %get-tuple-element.22, bf16[64,768]{1,0:T(8,128)(2,1)S(1)} %collective-permute-done.24, bf16[64,768]{1,0:T(8,128)(2,1)S(1)} %collective-permute-done.23, bf16[64,768]{1,0:T(8,128)(2,1)S(1)} %collective-permute-done.21, ...), kind=kLoop, calls=%fused_computation.6 | loop fusion | flops 552960 | bytes 921600 | tf_op jit(solution)/shard_map/convert_element_type | solution.py:274
  (21 shorter events, 0.0 us)
Async XLA Ops:
  0.0 9.4 %copy-start.4 = (f32[1440]{0:T(1024)S(1)}, f32[1440]{0:T(1024)}, u32[]{:S(2)}) copy-start(f32[1440]{0:T(1024)} %param.19) | copy-start | bytes 17284
  0.0 10.5 %copy-start.3 = (bf16[64,1440]{1,0:T(8,128)(2,1)S(1)}, bf16[64,1440]{1,0:T(8,128)(2,1)}, u32[]{:S(2)}) copy-start(bf16[64,1440]{1,0:T(8,128)(2,1)} %resid.1) | copy-start | bytes 552964
  0.0 29.0 %copy-start = (bf16[1,1440,720]{2,1,0:T(8,128)(2,1)S(1)}, bf16[1,1440,720]{2,1,0:T(8,128)(2,1)}, u32[]{:S(2)}) copy-start(bf16[1,1440,720]{2,1,0:T(8,128)(2,1)} %param.21) | copy-start | bytes 6220804
  0.0 29.0 %copy-start.1 = (bf16[1,1440,720]{2,1,0:T(8,128)(2,1)S(1)}, bf16[1,1440,720]{2,1,0:T(8,128)(2,1)}, u32[]{:S(2)}) copy-start(bf16[1,1440,720]{2,1,0:T(8,128)(2,1)} %param.22) | copy-start | bytes 6220804
  0.0 29.0 %copy-start.2 = (bf16[1,720,1440]{2,1,0:T(8,128)(2,1)S(1)}, bf16[1,720,1440]{2,1,0:T(8,128)(2,1)}, u32[]{:S(2)}) copy-start(bf16[1,720,1440]{2,1,0:T(8,128)(2,1)} %param.23) | copy-start | bytes 6220804
  8.8 1.6 %collective-permute-start = (bf16[64,1440]{1,0:T(8,128)(2,1)S(1)}, bf16[64,1440]{1,0:T(8,128)(2,1)S(1)}, u32[]{:S(2)}, u32[]{:S(2)}) collective-permute-start(bf16[64,1440]{1,0:T(8,128)(2,1)S(1)} %get-tuple-element.18), channel_id=1, source_target_pairs={{0,1},{1,0},{2,3},{3,2},{4,5},{5,4},{6,7},{7,6},{8,9},{9,8},{10,11... | collective-permute-start | bytes 552968 | tf_op jit(solution)/shard_map/ppermute | solution.py:242
  10.7 9.6 %collective-permute-start.5 = (bf16[32,1536]{1,0:T(8,128)(2,1)S(1)}, bf16[32,1536]{1,0:T(8,128)(2,1)S(1)}, u32[]{:S(2)}, u32[]{:S(2)}) collective-permute-start(bf16[32,1536]{1,0:T(8,128)(2,1)S(1)} %get-tuple-element.24), channel_id=1, source_target_pairs={{0,8},{2,10},{4,12},{6,14},{8,0},{10,2},{12,4},{14,6},{1,9},{3,11}... | collective-permute-start | bytes 294920 | tf_op jit(solution)/shard_map/ppermute | solution.py:242
  14.7 8.2 %collective-permute-start.2 = (bf16[32,1536]{1,0:T(8,128)(2,1)S(1)}, bf16[32,1536]{1,0:T(8,128)(2,1)S(1)}, u32[]{:S(2)}, u32[]{:S(2)}) collective-permute-start(bf16[32,1536]{1,0:T(8,128)(2,1)S(1)} %get-tuple-element.24), channel_id=1, source_target_pairs={{0,4},{2,6},{4,0},{6,2},{8,12},{10,14},{12,8},{14,10},{1,5},{3,7},... | collective-permute-start | bytes 294920 | tf_op jit(solution)/shard_map/ppermute | solution.py:242
  16.3 8.0 %collective-permute-start.10 = (bf16[32,1536]{1,0:T(8,128)(2,1)S(1)}, bf16[32,1536]{1,0:T(8,128)(2,1)S(1)}, u32[]{:S(2)}, u32[]{:S(2)}) collective-permute-start(bf16[32,1536]{1,0:T(8,128)(2,1)S(1)} %get-tuple-element.24), channel_id=1, source_target_pairs={{0,14},{2,12},{4,10},{6,8},{8,6},{10,4},{12,2},{14,0},{1,15},{3,13... | collective-permute-start | bytes 294920 | tf_op jit(solution)/shard_map/ppermute | solution.py:242
  20.3 6.2 %collective-permute-start.6 = (bf16[32,1536]{1,0:T(8,128)(2,1)S(1)}, bf16[32,1536]{1,0:T(8,128)(2,1)S(1)}, u32[]{:S(2)}, u32[]{:S(2)}) collective-permute-start(bf16[32,1536]{1,0:T(8,128)(2,1)S(1)} %collective-permute-done.5.refs_4_), channel_id=1, source_target_pairs={{0,2},{2,0},{4,6},{6,4},{8,10},{10,8},{12,14},{14,12},{1,3},{3,1},... | collective-permute-start | bytes 294920 | tf_op jit(solution)/shard_map/ppermute | solution.py:242
  22.9 4.6 %collective-permute-start.8 = (bf16[32,1536]{1,0:T(8,128)(2,1)S(1)}, bf16[32,1536]{1,0:T(8,128)(2,1)S(1)}, u32[]{:S(2)}, u32[]{:S(2)}) collective-permute-start(bf16[32,1536]{1,0:T(8,128)(2,1)S(1)} %collective-permute-done.5.refs_4_), channel_id=1, source_target_pairs={{0,4},{2,6},{4,0},{6,2},{8,12},{10,14},{12,8},{14,10},{1,5},{3,7},... | collective-permute-start | bytes 294920 | tf_op jit(solution)/shard_map/ppermute | solution.py:242
  22.9 4.9 %collective-permute-start.3 = (bf16[32,1536]{1,0:T(8,128)(2,1)S(1)}, bf16[32,1536]{1,0:T(8,128)(2,1)S(1)}, u32[]{:S(2)}, u32[]{:S(2)}) collective-permute-start(bf16[32,1536]{1,0:T(8,128)(2,1)S(1)} %collective-permute-done.2.refs_2_), channel_id=1, source_target_pairs={{0,2},{2,0},{4,6},{6,4},{8,10},{10,8},{12,14},{14,12},{1,3},{3,1},... | collective-permute-start | bytes 294920 | tf_op jit(solution)/shard_map/ppermute | solution.py:242
  24.3 3.7 %collective-permute-start.11 = (bf16[32,1536]{1,0:T(8,128)(2,1)S(1)}, bf16[32,1536]{1,0:T(8,128)(2,1)S(1)}, u32[]{:S(2)}, u32[]{:S(2)}) collective-permute-start(bf16[32,1536]{1,0:T(8,128)(2,1)S(1)} %collective-permute-done.10.refs_6_), channel_id=1, source_target_pairs={{0,1},{1,0},{2,3},{3,2},{4,5},{5,4},{6,7},{7,6},{8,9},{9,8},{10,11... | collective-permute-start | bytes 294920 | tf_op jit(solution)/shard_map/ppermute | solution.py:242
  26.5 1.5 %collective-permute-start.7 = (bf16[32,1536]{1,0:T(8,128)(2,1)S(1)}, bf16[32,1536]{1,0:T(8,128)(2,1)S(1)}, u32[]{:S(2)}, u32[]{:S(2)}) collective-permute-start(bf16[32,1536]{1,0:T(8,128)(2,1)S(1)} %collective-permute-done.6.refs_2_), channel_id=1, source_target_pairs={{0,1},{1,0},{2,3},{3,2},{4,5},{5,4},{6,7},{7,6},{8,9},{9,8},{10,11... | collective-permute-start | bytes 294920 | tf_op jit(solution)/shard_map/ppermute | solution.py:242
  27.5 1.3 %collective-permute-start.9 = (bf16[32,1536]{1,0:T(8,128)(2,1)S(1)}, bf16[32,1536]{1,0:T(8,128)(2,1)S(1)}, u32[]{:S(2)}, u32[]{:S(2)}) collective-permute-start(bf16[32,1536]{1,0:T(8,128)(2,1)S(1)} %collective-permute-done.8.refs_4_), channel_id=1, source_target_pairs={{0,1},{1,0},{2,3},{3,2},{4,5},{5,4},{6,7},{7,6},{8,9},{9,8},{10,11... | collective-permute-start | bytes 294920 | tf_op jit(solution)/shard_map/ppermute | solution.py:242
  27.7 1.3 %collective-permute-start.4 = (bf16[32,1536]{1,0:T(8,128)(2,1)S(1)}, bf16[32,1536]{1,0:T(8,128)(2,1)S(1)}, u32[]{:S(2)}, u32[]{:S(2)}) collective-permute-start(bf16[32,1536]{1,0:T(8,128)(2,1)S(1)} %collective-permute-done.3.refs_0_), channel_id=1, source_target_pairs={{0,1},{1,0},{2,3},{3,2},{4,5},{5,4},{6,7},{7,6},{8,9},{9,8},{10,11... | collective-permute-start | bytes 294920 | tf_op jit(solution)/shard_map/ppermute | solution.py:242
  31.4 8.6 %collective-permute-start.12 = (bf16[256,768]{1,0:T(8,128)(2,1)S(1)}, bf16[256,768]{1,0:T(8,128)(2,1)S(1)}, u32[]{:S(2)}, u32[]{:S(2)}) collective-permute-start(bf16[256,768]{1,0:T(8,128)(2,1)S(1)} %get-tuple-element.26), channel_id=1, source_target_pairs={{0,1},{1,0},{2,3},{3,2},{4,5},{5,4},{6,7},{7,6},{8,9},{9,8},{10,11... | collective-permute-start | bytes 1179656 | tf_op jit(solution)/shard_map/ppermute | solution.py:242
  31.7 5.0 %collective-permute-start.14 = (bf16[32,1536]{1,0:T(8,128)(2,1)S(1)}, bf16[32,1536]{1,0:T(8,128)(2,1)S(1)}, u32[]{:S(2)}, u32[]{:S(2)}) collective-permute-start(bf16[32,1536]{1,0:T(8,128)(2,1)S(1)} %get-tuple-element.24), channel_id=1, source_target_pairs={{0,2},{2,0},{4,6},{6,4},{8,10},{10,8},{12,14},{14,12},{1,3},{3,1},... | collective-permute-start | bytes 294920 | tf_op jit(solution)/shard_map/ppermute | solution.py:242
  32.9 3.8 %collective-permute-start.17 = (bf16[32,1536]{1,0:T(8,128)(2,1)S(1)}, bf16[32,1536]{1,0:T(8,128)(2,1)S(1)}, u32[]{:S(2)}, u32[]{:S(2)}) collective-permute-start(bf16[32,1536]{1,0:T(8,128)(2,1)S(1)} %collective-permute-done.5.refs_4_), channel_id=1, source_target_pairs={{0,1},{1,0},{2,3},{3,2},{4,5},{5,4},{6,7},{7,6},{8,9},{9,8},{10,11... | collective-permute-start | bytes 294920 | tf_op jit(solution)/shard_map/ppermute | solution.py:242
  33.0 3.7 %collective-permute-start.16 = (bf16[32,1536]{1,0:T(8,128)(2,1)S(1)}, bf16[32,1536]{1,0:T(8,128)(2,1)S(1)}, u32[]{:S(2)}, u32[]{:S(2)}) collective-permute-start(bf16[32,1536]{1,0:T(8,128)(2,1)S(1)} %collective-permute-done.2.refs_2_), channel_id=1, source_target_pairs={{0,1},{1,0},{2,3},{3,2},{4,5},{5,4},{6,7},{7,6},{8,9},{9,8},{10,11... | collective-permute-start | bytes 294920 | tf_op jit(solution)/shard_map/ppermute | solution.py:242
  36.6 1.3 %collective-permute-start.15 = (bf16[32,1536]{1,0:T(8,128)(2,1)S(1)}, bf16[32,1536]{1,0:T(8,128)(2,1)S(1)}, u32[]{:S(2)}, u32[]{:S(2)}) collective-permute-start(bf16[32,1536]{1,0:T(8,128)(2,1)S(1)} %collective-permute-done.14.refs_0_), channel_id=1, source_target_pairs={{0,1},{1,0},{2,3},{3,2},{4,5},{5,4},{6,7},{7,6},{8,9},{9,8},{10,11... | collective-permute-start | bytes 294920 | tf_op jit(solution)/shard_map/ppermute | solution.py:242
  39.8 5.7 %collective-permute-start.18 = (bf16[192,768]{1,0:T(8,128)(2,1)S(1)}, bf16[192,768]{1,0:T(8,128)(2,1)S(1)}, u32[]{:S(2)}, u32[]{:S(2)}) collective-permute-start(bf16[192,768]{1,0:T(8,128)(2,1)S(1)} %get-tuple-element.28), channel_id=1, source_target_pairs={{0,1},{1,0},{2,3},{3,2},{4,5},{5,4},{6,7},{7,6},{8,9},{9,8},{10,11... | collective-permute-start | bytes 884744 | tf_op jit(solution)/shard_map/ppermute | solution.py:242
  40.1 8.4 %collective-permute-start.19 = (bf16[64,768]{1,0:T(8,128)(2,1)S(1)}, bf16[64,768]{1,0:T(8,128)(2,1)S(1)}, u32[]{:S(2)}, u32[]{:S(2)}) collective-permute-start(bf16[64,768]{1,0:T(8,128)(2,1)S(1)} %get-tuple-element.32), channel_id=1, source_target_pairs={{0,4},{2,6},{4,0},{6,2},{8,12},{10,14},{12,8},{14,10},{1,5},{3,7},... | collective-permute-start | bytes 294920 | tf_op jit(solution)/shard_map/ppermute | solution.py:242
  41.9 6.6 %collective-permute-start.20 = (bf16[64,768]{1,0:T(8,128)(2,1)S(1)}, bf16[64,768]{1,0:T(8,128)(2,1)S(1)}, u32[]{:S(2)}, u32[]{:S(2)}) collective-permute-start(bf16[64,768]{1,0:T(8,128)(2,1)S(1)} %get-tuple-element.31), channel_id=1, source_target_pairs={{0,2},{2,0},{4,6},{6,4},{8,10},{10,8},{12,14},{14,12},{1,3},{3,1},... | collective-permute-start | bytes 294920 | tf_op jit(solution)/shard_map/ppermute | solution.py:242
  42.2 6.6 %collective-permute-start.22 = (bf16[64,768]{1,0:T(8,128)(2,1)S(1)}, bf16[64,768]{1,0:T(8,128)(2,1)S(1)}, u32[]{:S(2)}, u32[]{:S(2)}) collective-permute-start(bf16[64,768]{1,0:T(8,128)(2,1)S(1)} %get-tuple-element.30), channel_id=1, source_target_pairs={{0,2},{2,0},{4,6},{6,4},{8,10},{10,8},{12,14},{14,12},{1,3},{3,1},... | collective-permute-start | bytes 294920 | tf_op jit(solution)/shard_map/ppermute | solution.py:242
  45.4 7.7 %collective-permute-start.1 = (bf16[64,768]{1,0:T(8,128)(2,1)S(1)}, bf16[64,768]{1,0:T(8,128)(2,1)S(1)}, u32[]{:S(2)}, u32[]{:S(2)}) collective-permute-start(bf16[64,768]{1,0:T(8,128)(2,1)S(1)} %get-tuple-element.23), channel_id=1, source_target_pairs={{0,1},{1,0},{2,3},{3,2},{4,5},{5,4},{6,7},{7,6},{8,9},{9,8},{10,11... | collective-permute-start | bytes 294920 | tf_op jit(solution)/shard_map/ppermute | solution.py:242
  45.5 8.5 %collective-permute-start.13 = (bf16[64,768]{1,0:T(8,128)(2,1)S(1)}, bf16[64,768]{1,0:T(8,128)(2,1)S(1)}, u32[]{:S(2)}, u32[]{:S(2)}) collective-permute-start(bf16[64,768]{1,0:T(8,128)(2,1)S(1)} %get-tuple-element.29), channel_id=1, source_target_pairs={{0,14},{2,12},{4,10},{6,8},{8,6},{10,4},{12,2},{14,0},{1,15},{3,13... | collective-permute-start | bytes 294920 | tf_op jit(solution)/shard_map/ppermute | solution.py:242
  48.9 8.6 %collective-permute-start.21 = (bf16[64,768]{1,0:T(8,128)(2,1)S(1)}, bf16[64,768]{1,0:T(8,128)(2,1)S(1)}, u32[]{:S(2)}, u32[]{:S(2)}) collective-permute-start(bf16[64,768]{1,0:T(8,128)(2,1)S(1)} %get-tuple-element.33), channel_id=1, source_target_pairs={{0,8},{2,10},{4,12},{6,14},{8,0},{10,2},{12,4},{14,6},{1,9},{3,11}... | collective-permute-start | bytes 294920 | tf_op jit(solution)/shard_map/ppermute | solution.py:242
  51.1 6.5 %collective-permute-start.23 = (bf16[64,768]{1,0:T(8,128)(2,1)S(1)}, bf16[64,768]{1,0:T(8,128)(2,1)S(1)}, u32[]{:S(2)}, u32[]{:S(2)}) collective-permute-start(bf16[64,768]{1,0:T(8,128)(2,1)S(1)} %get-tuple-element.35), channel_id=1, source_target_pairs={{0,4},{2,6},{4,0},{6,2},{8,12},{10,14},{12,8},{14,10},{1,5},{3,7},... | collective-permute-start | bytes 294920 | tf_op jit(solution)/shard_map/ppermute | solution.py:242
  52.5 5.1 %collective-permute-start.24 = (bf16[64,768]{1,0:T(8,128)(2,1)S(1)}, bf16[64,768]{1,0:T(8,128)(2,1)S(1)}, u32[]{:S(2)}, u32[]{:S(2)}) collective-permute-start(bf16[64,768]{1,0:T(8,128)(2,1)S(1)} %get-tuple-element.34), channel_id=1, source_target_pairs={{0,2},{2,0},{4,6},{6,4},{8,10},{10,8},{12,14},{14,12},{1,3},{3,1},... | collective-permute-start | bytes 294920 | tf_op jit(solution)/shard_map/ppermute | solution.py:242
where the time goes:
time: 58.5 us; the launch traced here: 58.3 us
  starting transfers between devices  23.9 us (41%)
  waiting for transfers between devices  18.8 us (32%)
  Pallas kernels  14.6 us (25%)
  other arithmetic  0.88 us (2%)
    ppermute x25, starting transfers between devices, flip(): lax.ppermute(value, axis, [(i, i ^ offset) for i in range(lax.axis_size(a...  23.9 us
    ppermute x25, waiting for transfers between devices, flip(): lax.ppermute(value, axis, [(i, i ^ offset) for i in range(lax.axis_size(a...  18.8 us
    pallas_call x1, Pallas kernels, attend(): pl.pallas_call(functools.partial(attend_kernel, heads, min(16, tokens), e...  8.8 us
    pallas_call x3, Pallas kernels, expert(): pl.pallas_call(functools.partial(expert_kernel, experts, pieces), out_sha...  5.57 us
  transfers between devices with their start and end apart: 25, of which 14 were waited for; matrix products, arithmetic and copies ran while one was open for 0% of the time, Pallas kernels for 6%

commit v1 on v0

--- a/solution.py
+++ b/solution.py
@@ -12,6 +12,7 @@
 HEAD_WIDTH = 64
 LANES = 128
 MIB = 1 << 20
+ATTEND_MIB = 36
 
 SMEM = pl.BlockSpec(memory_space=pltpu.SMEM)
 VMEM = pl.BlockSpec(memory_space=pltpu.VMEM)
@@ -38,75 +39,71 @@
 
 def attend_kernel(
     heads,
-    unroll,
     experts,
-    table,
-    length,
-    q_ref,
+    table_in,
+    length_in,
+    q_in,
     pages,
     proj,
-    chosen,
-    logits,
-    out_wide,
-    out_sent,
-    out_gates,
-    kbuf,
-    vbuf,
-    wbuf,
-    qs,
-    os,
-    sem,
+    chosen_in,
+    logits_in,
+    *refs,
 ):
-    tokens = q_ref.shape[0]
+    count = (len(refs) - 15) // 2
+    weights_in, (out_wide, out_sent, out_gates) = refs[:count], refs[count : count + 3]
+    weights_out, refs = refs[count + 3 : 2 * count + 3], refs[2 * count + 3 :]
+    table, length, q, chosen, logits, kbuf, vbuf, wbuf, qs, ws, os, sem = refs
+    tokens = q.shape[0]
     per_token = table.shape[0]
     lanes = kbuf.shape[2]
     positions = per_token * kbuf.shape[1]
-    copies = [
-        pltpu.make_async_copy(pages.at[0], kbuf, sem.at[0]),
-        pltpu.make_async_copy(pages.at[1], vbuf, sem.at[1]),
-        pltpu.make_async_copy(proj, wbuf, sem.at[2]),
-    ]
+    moves = (
+        (q_in, q),
+        (chosen_in, chosen),
+        (logits_in, logits),
+        (table_in, table),
+        (length_in, length),
+        (pages.at[0], kbuf),
+        (pages.at[1], vbuf),
+        (proj, wbuf),
+        *zip(weights_in, weights_out),
+    )
+    copies = [pltpu.make_async_copy(*move, sem.at[i]) for i, move in enumerate(moves)]
+    small, (keys_in, values_in, proj_in), experts_in = copies[:5], copies[5:8], copies[8:]
     for copy in copies:
         copy.start()
+    small[0].wait()
     low = lax.broadcasted_iota(jnp.int32, (tokens, lanes), 1) < HEAD_WIDTH
     half = heads // 2
     for h in range(heads):
-        pair = q_ref[:, (h // 2) * lanes : (h // 2 + 1) * lanes].astype(jnp.float32)
+        pair = q[:, (h // 2) * lanes : (h // 2 + 1) * lanes].astype(jnp.float32)
         if (h < half) != (h % 2 == 0):
             pair = pltpu.roll(pair, HEAD_WIDTH, 1)
         row = jnp.where(low if h < half else ~low, pair, 0.0)
         qs[pl.ds(h, tokens, stride=heads), :] = row * (1.0 / math.sqrt(HEAD_WIDTH))
+    for copy in small[1:]:
+        copy.wait()
     dense_gates(experts, chosen, logits, out_gates)
-    copies[0].wait()
-    copies[1].wait()
+    keys_in.wait()
     spot = lax.broadcasted_iota(jnp.int32, (heads, positions), 1)
 
-    @pl.loop(0, tokens // unroll)
-    def _(step):
-        scores, values = [], []
-        for u in range(unroll):
-            t = step * unroll + u
-            ids = [table[i, t] for i in range(per_token)]
-            keys = jnp.concatenate([kbuf[i] for i in ids], axis=0)
-            values.append(jnp.concatenate([vbuf[i] for i in ids], axis=0))
-            q = qs[pl.ds(pl.multiple_of(t * heads, heads), heads), :].astype(jnp.bfloat16)
-            s = lax.dot_general(
-                q, keys, (((1,), (1,)), ((), ())), preferred_element_type=jnp.float32
-            )
-            scores.append(jnp.where(spot < length[t], s, -jnp.inf))
-        s = jnp.concatenate(scores, axis=0)
-        w = jnp.exp(s - jnp.max(s, axis=1, keepdims=True))
-        total = jnp.sum(w, axis=1, keepdims=True)
-        p = w.astype(jnp.bfloat16)
-        o = jnp.concatenate(
-            [
-                jnp.dot(p[u * heads : (u + 1) * heads], values[u], preferred_element_type=jnp.float32)
-                for u in range(unroll)
-            ],
-            axis=0,
+    def tiles(buffer, t):
+        return jnp.concatenate([buffer[table[i, t]] for i in range(per_token)], axis=0)
+
+    scores = []
+    for t in range(tokens):
+        rows = qs[t * heads : (t + 1) * heads, :].astype(jnp.bfloat16)
+        s = lax.dot_general(
+            rows, tiles(kbuf, t), (((1,), (1,)), ((), ())), preferred_element_type=jnp.float32
         )
-        rows = unroll * heads
-        os[pl.ds(pl.multiple_of(step * rows, rows), rows), :] = o / total
+        scores.append(jnp.where(spot < length[t], s, -jnp.inf))
+    s = jnp.concatenate(scores, axis=0)
+    w = jnp.exp(s - jnp.max(s, axis=1, keepdims=True))
+    ws[...] = (w / jnp.sum(w, axis=1, keepdims=True)).astype(jnp.bfloat16)
+    values_in.wait()
+    for t in range(tokens):
+        rows = slice(t * heads, (t + 1) * heads)
+        os[rows, :] = jnp.dot(ws[rows, :], tiles(vbuf, t), preferred_element_type=jnp.float32)
 
     parts = []
     for j in range(half):
@@ -118,40 +115,49 @@
             even = pltpu.roll(even, HEAD_WIDTH, 1)
         parts.append(jnp.where(low, even, odd).astype(jnp.bfloat16))
     attended = jnp.concatenate(parts, axis=1)
-    copies[2].wait()
+    proj_in.wait()
     part = lax.dot_general(
         attended, wbuf[...], (((1,), (1,)), ((), ())), preferred_element_type=jnp.float32
     )
     out_wide[...] = part
     out_sent[...] = part.astype(jnp.bfloat16)
-
-
-def attend(query, pages, page_table, ctx_len, out_proj, chosen, logits, experts):
+    for copy in experts_in:
+        copy.wait()
+
+
+def attend(query, pages, page_table, ctx_len, out_proj, chosen, logits, experts, weights):
     tokens = query.shape[0]
     heads = query.shape[1] // HEAD_WIDTH
     width = out_proj.shape[1]
     lanes = pages.shape[3]
     rows = (tokens * heads, lanes)
-    operands = (page_table.T, ctx_len, query, pages, out_proj.T, chosen.T, logits.T)
+    operands = (page_table.T, ctx_len, query, pages, out_proj.T, chosen.T, logits.T, *weights)
     operands = [pltpu.with_memory_space_constraint(v, pltpu.HBM) for v in operands]
     return pl.pallas_call(
-        functools.partial(attend_kernel, heads, min(16, tokens), experts),
+        functools.partial(attend_kernel, heads, experts),
         out_shape=(
             jax.ShapeDtypeStruct((tokens, width), jnp.float32),
             jax.ShapeDtypeStruct((tokens, width), jnp.bfloat16),
             jax.ShapeDtypeStruct((tokens, 2 * experts), jnp.bfloat16),
+            *[jax.ShapeDtypeStruct(w.shape, w.dtype) for w in weights],
         ),
-        in_specs=[SMEM, SMEM, VMEM, HBM, HBM, VMEM, VMEM],
-        out_specs=(VMEM,) * 3,
+        in_specs=[HBM] * len(operands),
+        out_specs=(VMEM,) * (3 + len(weights)),
         scratch_shapes=[
+            pltpu.SMEM(operands[0].shape, jnp.int32),
+            pltpu.SMEM(operands[1].shape, jnp.int32),
+            pltpu.VMEM(query.shape, query.dtype),
+            pltpu.VMEM(operands[5].shape, jnp.int32),
+            pltpu.VMEM(operands[6].shape, jnp.float32),
             pltpu.VMEM(pages.shape[1:], pages.dtype),
             pltpu.VMEM(pages.shape[1:], pages.dtype),
-            pltpu.VMEM(out_proj.shape[::-1], out_proj.dtype),
+            pltpu.VMEM(operands[4].shape, out_proj.dtype),
             pltpu.VMEM(rows, jnp.float32),
+            pltpu.VMEM((rows[0], page_table.shape[1] * pages.shape[2]), jnp.bfloat16),
             pltpu.VMEM(rows, jnp.float32),
-            pltpu.SemaphoreType.DMA((3,)),
+            pltpu.SemaphoreType.DMA((8 + len(weights),)),
         ],
-        compiler_params=pltpu.CompilerParams(vmem_limit_bytes=50 * MIB),
+        compiler_params=pltpu.CompilerParams(vmem_limit_bytes=ATTEND_MIB * MIB),
         name="attend",
     )(*operands)
 
@@ -246,7 +252,7 @@
     return 0 if k == owners - 1 else k & (k - 1)
 
 
-def routed_all(stream, whole, mine, w_gate, w_up, w_down, experts):
+def routed_all(stream, whole, mine, weights, experts):
     owners = lax.axis_size("ep")
     tokens = whole.shape[0]
     near = [k for k in range(1, owners) if k & (k - 1) == 0]
@@ -262,7 +268,7 @@
             sources = []
             for k in group:
                 sources += [half[k], flip(half[k], "tp", 1)]
-        kept, sent = expert(sources, w_gate[0], w_up[0], w_down[0], experts)
+        kept, sent = expert(sources, *weights, experts)
         received = flip(sent, "tp", 1)
         for i, k in enumerate(group):
             rows = slice(i * tokens, (i + 1) * tokens)
@@ -345,18 +351,27 @@
     capacity = max(2, min(tok_rows, 2 * tok_rows * top_count // experts))
     padded = -(-model_width // LANES) * LANES
 
-    own, sent, gates = attend(
-        query, key_value_pages, page_table, ctx_len, out_proj, experts_chosen, router_logits, experts
-    )
-    other = flip(sent, "tp", 1)
-    if (
+    dense = (
         local_experts == 1
         and tok_rows <= capacity
         and model_width + 2 * experts <= padded
         and owners & (owners - 1) == 0
-    ):
+    )
+    own, sent, gates, *weights = attend(
+        query,
+        key_value_pages,
+        page_table,
+        ctx_len,
+        out_proj,
+        experts_chosen,
+        router_logits,
+        experts,
+        (w_gate[0], w_up[0], w_down[0]) if dense else (),
+    )
+    other = flip(sent, "tp", 1)
+    if dense:
         stream, whole, mine = norm(resid, own, other, norm_gain, gates, padded)
-        return routed_all(stream, whole, mine, w_gate, w_up, w_down, experts)
+        return routed_all(stream, whole, mine, weights, experts)
     half_cols = model_width // lax.axis_size("tp")
     offset = lax.axis_index("tp") * half_cols
     stream = resid.astype(jnp.float32) + own + other.astype(jnp.float32)

time: 58.5 us -> 58.2 us (level)
  waiting for transfers between devices: 18.8 us -> 24.4 us
  starting transfers between devices: 23.9 us -> 20.5 us
  Pallas kernels: 14.6 us -> 12 us
    ppermute x25, waiting for transfers between devices: 18.8 us -> 24.4 us  [flip(): lax.ppermute(value, axis, [(i, i ^ offset) for i in range(lax.axis_size(a...]
    ppermute x25, starting transfers between devices: 23.9 us -> 20.5 us  [flip(): lax.ppermute(value, axis, [(i, i ^ offset) for i in range(lax.axis_size(a...]
    pallas_call x1, Pallas kernels: 8.8 us -> 6.22 us  [attend(): pl.pallas_call(functools.partial(attend_kernel, heads, experts), out_shap...]
  transfers between devices with their start and end apart: 25 -> 25, of which waited for: 14 -> 13; matrix products, arithmetic and copies ran while one was open for 0% -> 0% of each run, Pallas kernels for 6% -> 6%
where the time goes in v1:
time: 58.2 us; the launch traced here: 58 us
  waiting for transfers between devices  24.4 us (42%)
  starting transfers between devices  20.5 us (35%)
  Pallas kernels  12 us (21%)
  other arithmetic  0.89 us (2%)
    ppermute x25, waiting for transfers between devices, flip(): lax.ppermute(value, axis, [(i, i ^ offset) for i in range(lax.axis_size(a...  24.4 us
    ppermute x25, starting transfers between devices, flip(): lax.ppermute(value, axis, [(i, i ^ offset) for i in range(lax.axis_size(a...  20.5 us
    pallas_call x1, Pallas kernels, attend(): pl.pallas_call(functools.partial(attend_kernel, heads, experts), out_shap...  6.22 us
    pallas_call x3, Pallas kernels, expert(): pl.pallas_call(functools.partial(expert_kernel, experts, pieces), out_sha...  5.57 us
  transfers between devices with their start and end apart: 25, of which 13 were waited for; matrix products, arithmetic and copies ran while one was open for 0% of the time, Pallas kernels for 6%

profile of v1, /device:TPU:0, one launch (start us, length us, event | category | flops | bytes accessed | tf_op | source)
XLA Modules:
  0.0 58.0 jit_solution(6643939099405384007)
XLA Ops:
  0.0 6.2 %attend.1 = (f32[64,1440]{1,0:T(8,128)S(1)}, bf16[64,1440]{1,0:T(8,128)(2,1)S(1)}, bf16[64,16]{1,0:T(8,128)(2,1)S(1)}, bf16[1440,720]{1,0:T(8,128)(2,1)S(1)}, bf...) custom-call(s32[12,64]{1,0:T(8,128)} %bitcast.11, s32[64]{0:T(128)} %length_in.1, bf16[64,1024]{1,0:T(8,128)(2,1)} %q_in.1, ...), custom_call_target="tpu_custom_call" | custom-call | tf_op jit(solution)/shard_map/attend/pallas_call | solution.py:136
  6.2 0.6 collective-permute-start
  6.8 1.1 %collective-permute-done.other = bf16[64,1440]{1,0:T(8,128)(2,1)S(1)} collective-permute-done((bf16[64,1440]{1,0:T(8,128)(2,1)S(1)}, bf16[64,1440]{1,0:T(8,128)(2,1)S(1)}, u32[]{:S(2)}, u32[]{:S(2)}) %collective-permute-start) | collective-permute-done | bytes 184352 | tf_op jit(solution)/shard_map/ppermute | solution.py:248
  7.9 0.2 norm.1
  8.1 3.0 %collective-permute-start.2 = (bf16[32,1536]{1,0:T(8,128)(2,1)S(1)}, bf16[32,1536]{1,0:T(8,128)(2,1)S(1)}, u32[]{:S(2)}, u32[]{:S(2)}) collective-permute-start(bf16[32,1536]{1,0:T(8,128)(2,1)S(1)} %get-tuple-element.30), channel_id=1, source_target_pairs={{0,4},{2,6},{4,0},{6,2},{8,12},{10,14},{12,8},{14,10},{1,5},{3,7},... | collective-permute-start | bytes 294920 | tf_op jit(solution)/shard_map/ppermute | solution.py:248
  11.1 2.6 %collective-permute-start.5 = (bf16[32,1536]{1,0:T(8,128)(2,1)S(1)}, bf16[32,1536]{1,0:T(8,128)(2,1)S(1)}, u32[]{:S(2)}, u32[]{:S(2)}) collective-permute-start(bf16[32,1536]{1,0:T(8,128)(2,1)S(1)} %get-tuple-element.30), channel_id=1, source_target_pairs={{0,8},{2,10},{4,12},{6,14},{8,0},{10,2},{12,4},{14,6},{1,9},{3,11}... | collective-permute-start | bytes 294920 | tf_op jit(solution)/shard_map/ppermute | solution.py:248
  13.7 1.2 %collective-permute-start.10 = (bf16[32,1536]{1,0:T(8,128)(2,1)S(1)}, bf16[32,1536]{1,0:T(8,128)(2,1)S(1)}, u32[]{:S(2)}, u32[]{:S(2)}) collective-permute-start(bf16[32,1536]{1,0:T(8,128)(2,1)S(1)} %get-tuple-element.30), channel_id=1, source_target_pairs={{0,14},{2,12},{4,10},{6,8},{8,6},{10,4},{12,2},{14,0},{1,15},{3,13... | collective-permute-start | bytes 294920 | tf_op jit(solution)/shard_map/ppermute | solution.py:248
  14.8 1.0 %collective-permute-start.3 = (bf16[32,1536]{1,0:T(8,128)(2,1)S(1)}, bf16[32,1536]{1,0:T(8,128)(2,1)S(1)}, u32[]{:S(2)}, u32[]{:S(2)}) collective-permute-start(bf16[32,1536]{1,0:T(8,128)(2,1)S(1)} %collective-permute-done.2.refs_2_), channel_id=1, source_target_pairs={{0,2},{2,0},{4,6},{6,4},{8,10},{10,8},{12,14},{14,12},{1,3},{3,1},... | collective-permute-start | bytes 294920 | tf_op jit(solution)/shard_map/ppermute | solution.py:248
  15.9 5.5 %collective-permute-done.5.refs_4_ = bf16[32,1536]{1,0:T(8,128)(2,1)S(1)} collective-permute-done((bf16[32,1536]{1,0:T(8,128)(2,1)S(1)}, bf16[32,1536]{1,0:T(8,128)(2,1)S(1)}, u32[]{:S(2)}, u32[]{:S(2)}) %collective-permute-start.5) | collective-permute-done | bytes 98336 | tf_op jit(solution)/shard_map/ppermute | solution.py:248
  21.3 2.0 %collective-permute-start.6 = (bf16[32,1536]{1,0:T(8,128)(2,1)S(1)}, bf16[32,1536]{1,0:T(8,128)(2,1)S(1)}, u32[]{:S(2)}, u32[]{:S(2)}) collective-permute-start(bf16[32,1536]{1,0:T(8,128)(2,1)S(1)} %collective-permute-done.5.refs_4_), channel_id=1, source_target_pairs={{0,2},{2,0},{4,6},{6,4},{8,10},{10,8},{12,14},{14,12},{1,3},{3,1},... | collective-permute-start | bytes 294920 | tf_op jit(solution)/shard_map/ppermute | solution.py:248
  23.3 0.0 collective-permute-start.8
  23.3 0.0 collective-permute-done.10.refs_6_
  23.3 0.0 collective-permute-done.3.refs_0_
  23.3 0.5 collective-permute-start.4
  23.8 2.1 %collective-permute-done.6.refs_2_ = bf16[32,1536]{1,0:T(8,128)(2,1)S(1)} collective-permute-done((bf16[32,1536]{1,0:T(8,128)(2,1)S(1)}, bf16[32,1536]{1,0:T(8,128)(2,1)S(1)}, u32[]{:S(2)}, u32[]{:S(2)}) %collective-permute-start.6) | collective-permute-done | bytes 98336 | tf_op jit(solution)/shard_map/ppermute | solution.py:248
  25.9 0.0 collective-permute-start.7
  25.9 2.0 %collective-permute-done.8.refs_4_ = bf16[32,1536]{1,0:T(8,128)(2,1)S(1)} collective-permute-done((bf16[32,1536]{1,0:T(8,128)(2,1)S(1)}, bf16[32,1536]{1,0:T(8,128)(2,1)S(1)}, u32[]{:S(2)}, u32[]{:S(2)}) %collective-permute-start.8) | collective-permute-done | bytes 98336 | tf_op jit(solution)/shard_map/ppermute | solution.py:248
  27.9 0.0 collective-permute-done.11.refs_7_
  27.9 0.0 collective-permute-done.4.refs_1_
  27.9 0.0 collective-permute-done.7.refs_3_
  27.9 1.3 %collective-permute-done.9.refs_5_ = bf16[32,1536]{1,0:T(8,128)(2,1)S(1)} collective-permute-done((bf16[32,1536]{1,0:T(8,128)(2,1)S(1)}, bf16[32,1536]{1,0:T(8,128)(2,1)S(1)}, u32[]{:S(2)}, u32[]{:S(2)}) %collective-permute-start.9) | collective-permute-done | bytes 98336 | tf_op jit(solution)/shard_map/ppermute | solution.py:248
  29.2 2.3 %expert.4 = (f32[256,768]{1,0:T(8,128)S(1)}, bf16[256,768]{1,0:T(8,128)(2,1)S(1)}) custom-call(bf16[32,1536]{1,0:T(8,128)(2,1)S(1)} %collective-permute-done.3.refs_0_, bf16[32,1536]{1,0:T(8,128)(2,1)S(1)} %collective-permute-done.4.refs_1_, bf16[32,1536]{1,0:T(8,128)(2,1)S(1)} %collective-permute-done.6.refs_2_, ...), custom_call_target="tpu_custom_call" | custom-call | flops 1592524800 | bytes 6220800 | tf_op jit(solution)/shard_map/expert/pallas_call | solution.py:230
  31.5 0.2 collective-permute-start.12
  31.7 0.4 collective-permute-start.14
  32.1 4.7 %collective-permute-done.14.refs_0_ = bf16[32,1536]{1,0:T(8,128)(2,1)S(1)} collective-permute-done((bf16[32,1536]{1,0:T(8,128)(2,1)S(1)}, bf16[32,1536]{1,0:T(8,128)(2,1)S(1)}, u32[]{:S(2)}, u32[]{:S(2)}) %collective-permute-start.14) | collective-permute-done | bytes 98336 | tf_op jit(solution)/shard_map/ppermute | solution.py:248
  36.8 0.5 collective-permute-start.16
  37.3 0.0 collective-permute-start.17
  37.3 0.8 %collective-permute-done.15.refs_1_ = bf16[32,1536]{1,0:T(8,128)(2,1)S(1)} collective-permute-done((bf16[32,1536]{1,0:T(8,128)(2,1)S(1)}, bf16[32,1536]{1,0:T(8,128)(2,1)S(1)}, u32[]{:S(2)}, u32[]{:S(2)}) %collective-permute-start.15) | collective-permute-done | bytes 98336 | tf_op jit(solution)/shard_map/ppermute | solution.py:248
  38.1 0.2 collective-permute-done.16.refs_3_
  38.2 0.4 collective-permute-done.17.refs_5_
  38.6 1.8 %expert.5 = (f32[192,768]{1,0:T(8,128)S(1)}, bf16[192,768]{1,0:T(8,128)(2,1)S(1)}) custom-call(bf16[32,1536]{1,0:T(8,128)(2,1)S(1)} %collective-permute-done.14.refs_0_, bf16[32,1536]{1,0:T(8,128)(2,1)S(1)} %collective-permute-done.15.refs_1_, bf16[32,1536]{1,0:T(8,128)(2,1)S(1)} %collective-permute-done.2.refs_2_, ...), custom_call_target="tpu_custom_call" | custom-call | flops 1194393600 | bytes 6220800 | tf_op jit(solution)/shard_map/expert/pallas_call | solution.py:230
  40.4 0.2 collective-permute-start.18
  40.7 0.0 collective-permute-done.12
  40.7 0.1 add_convert_fusion.6
  40.7 0.3 collective-permute-start.20
  41.1 1.7 %collective-permute-start.22 = (bf16[64,768]{1,0:T(8,128)(2,1)S(1)}, bf16[64,768]{1,0:T(8,128)(2,1)S(1)}, u32[]{:S(2)}, u32[]{:S(2)}) collective-permute-start(bf16[64,768]{1,0:T(8,128)(2,1)S(1)} %get-tuple-element.36), channel_id=1, source_target_pairs={{0,2},{2,0},{4,6},{6,4},{8,10},{10,8},{12,14},{14,12},{1,3},{3,1},... | collective-permute-start | bytes 294920 | tf_op jit(solution)/shard_map/ppermute | solution.py:248
  42.8 1.4 %expert.3 = (f32[64,768]{1,0:T(8,128)S(1)}, bf16[64,768]{1,0:T(8,128)(2,1)S(1)}) custom-call(bf16[64,1536]{1,0:T(8,128)(2,1)S(1)} %get-tuple-element.24.refs_0_, bf16[1440,720]{1,0:T(8,128)(2,1)S(1)} %get-tuple-element.25.refs_1_.refs_8_.refs_6_, bf16[1440,720]{1,0:T(8,128)(2,1)S(1)} %get-tuple-element.26.refs_2_.refs_9_.refs_7_, ...), custom_call_target="tpu_custom_call" | custom-call | flops 398131200 | bytes 6220800 | tf_op jit(solution)/shard_map/expert/pallas_call | solution.py:230
  44.3 0.1 collective-permute-start.1
  44.4 2.6 %collective-permute-start.13 = (bf16[64,768]{1,0:T(8,128)(2,1)S(1)}, bf16[64,768]{1,0:T(8,128)(2,1)S(1)}, u32[]{:S(2)}, u32[]{:S(2)}) collective-permute-start(bf16[64,768]{1,0:T(8,128)(2,1)S(1)} %get-tuple-element.35), channel_id=1, source_target_pairs={{0,14},{2,12},{4,10},{6,8},{8,6},{10,4},{12,2},{14,0},{1,15},{3,13... | collective-permute-start | bytes 294920 | tf_op jit(solution)/shard_map/ppermute | solution.py:248
  47.0 1.0 %collective-permute-done.22 = bf16[64,768]{1,0:T(8,128)(2,1)S(1)} collective-permute-done((bf16[64,768]{1,0:T(8,128)(2,1)S(1)}, bf16[64,768]{1,0:T(8,128)(2,1)S(1)}, u32[]{:S(2)}, u32[]{:S(2)}) %collective-permute-start.22) | collective-permute-done | bytes 98336 | tf_op jit(solution)/shard_map/ppermute | solution.py:248
  48.0 0.1 add_convert_fusion.3
  48.1 0.6 collective-permute-start.24
  48.6 1.1 %collective-permute-start.23 = (bf16[64,768]{1,0:T(8,128)(2,1)S(1)}, bf16[64,768]{1,0:T(8,128)(2,1)S(1)}, u32[]{:S(2)}, u32[]{:S(2)}) collective-permute-start(bf16[64,768]{1,0:T(8,128)(2,1)S(1)} %get-tuple-element.41), channel_id=1, source_target_pairs={{0,4},{2,6},{4,0},{6,2},{8,12},{10,14},{12,8},{14,10},{1,5},{3,7},... | collective-permute-start | bytes 294920 | tf_op jit(solution)/shard_map/ppermute | solution.py:248
  49.7 2.0 %collective-permute-start.21 = (bf16[64,768]{1,0:T(8,128)(2,1)S(1)}, bf16[64,768]{1,0:T(8,128)(2,1)S(1)}, u32[]{:S(2)}, u32[]{:S(2)}) collective-permute-start(bf16[64,768]{1,0:T(8,128)(2,1)S(1)} %get-tuple-element.39), channel_id=1, source_target_pairs={{0,8},{2,10},{4,12},{6,14},{8,0},{10,2},{12,4},{14,6},{1,9},{3,11}... | collective-permute-start | bytes 294920 | tf_op jit(solution)/shard_map/ppermute | solution.py:248
  51.8 0.7 %collective-permute-done.13 = bf16[64,768]{1,0:T(8,128)(2,1)S(1)} collective-permute-done((bf16[64,768]{1,0:T(8,128)(2,1)S(1)}, bf16[64,768]{1,0:T(8,128)(2,1)S(1)}, u32[]{:S(2)}, u32[]{:S(2)}) %collective-permute-start.13) | collective-permute-done | bytes 98336 | tf_op jit(solution)/shard_map/ppermute | solution.py:248
  52.5 1.9 %collective-permute-done.24 = bf16[64,768]{1,0:T(8,128)(2,1)S(1)} collective-permute-done((bf16[64,768]{1,0:T(8,128)(2,1)S(1)}, bf16[64,768]{1,0:T(8,128)(2,1)S(1)}, u32[]{:S(2)}, u32[]{:S(2)}) %collective-permute-start.24) | collective-permute-done | bytes 98336 | tf_op jit(solution)/shard_map/ppermute | solution.py:248
  54.4 2.9 %collective-permute-done.21 = bf16[64,768]{1,0:T(8,128)(2,1)S(1)} collective-permute-done((bf16[64,768]{1,0:T(8,128)(2,1)S(1)}, bf16[64,768]{1,0:T(8,128)(2,1)S(1)}, u32[]{:S(2)}, u32[]{:S(2)}) %collective-permute-start.21) | collective-permute-done | bytes 98336 | tf_op jit(solution)/shard_map/ppermute | solution.py:248
  57.3 0.7 %fusion.5 = bf16[64,720]{1,0:T(8,128)(2,1)} fusion(f32[64,720]{1,0:T(8,128)S(1)} %get-tuple-element.23, f32[64,768]{1,0:T(8,128)S(1)} %get-tuple-element.28, bf16[64,768]{1,0:T(8,128)(2,1)S(1)} %collective-permute-done.24, bf16[64,768]{1,0:T(8,128)(2,1)S(1)} %collective-permute-done.23, bf16[64,768]{1,0:T(8,128)(2,1)S(1)} %collective-permute-done.21, ...), kind=kLoop, calls=%fused_computation.6 | loop fusion | flops 552960 | bytes 921600 | tf_op jit(solution)/shard_map/convert_element_type | solution.py:280
  (15 shorter events, 0.0 us)
Async XLA Ops:
  0.0 6.8 %copy-start.1 = (f32[1440]{0:T(1024)S(1)}, f32[1440]{0:T(1024)}, u32[]{:S(2)}) copy-start(f32[1440]{0:T(1024)} %param.19) | copy-start | bytes 17284
  0.0 7.9 %copy-start = (bf16[64,1440]{1,0:T(8,128)(2,1)S(1)}, bf16[64,1440]{1,0:T(8,128)(2,1)}, u32[]{:S(2)}) copy-start(bf16[64,1440]{1,0:T(8,128)(2,1)} %resid.1) | copy-start | bytes 552964
  6.2 1.6 %collective-permute-start = (bf16[64,1440]{1,0:T(8,128)(2,1)S(1)}, bf16[64,1440]{1,0:T(8,128)(2,1)S(1)}, u32[]{:S(2)}, u32[]{:S(2)}) collective-permute-start(bf16[64,1440]{1,0:T(8,128)(2,1)S(1)} %get-tuple-element.21), channel_id=1, source_target_pairs={{0,1},{1,0},{2,3},{3,2},{4,5},{5,4},{6,7},{7,6},{8,9},{9,8},{10,11... | collective-permute-start | bytes 552968 | tf_op jit(solution)/shard_map/ppermute | solution.py:248
  8.1 6.7 %collective-permute-start.2 = (bf16[32,1536]{1,0:T(8,128)(2,1)S(1)}, bf16[32,1536]{1,0:T(8,128)(2,1)S(1)}, u32[]{:S(2)}, u32[]{:S(2)}) collective-permute-start(bf16[32,1536]{1,0:T(8,128)(2,1)S(1)} %get-tuple-element.30), channel_id=1, source_target_pairs={{0,4},{2,6},{4,0},{6,2},{8,12},{10,14},{12,8},{14,10},{1,5},{3,7},... | collective-permute-start | bytes 294920 | tf_op jit(solution)/shard_map/ppermute | solution.py:248
  11.1 10.2 %collective-permute-start.5 = (bf16[32,1536]{1,0:T(8,128)(2,1)S(1)}, bf16[32,1536]{1,0:T(8,128)(2,1)S(1)}, u32[]{:S(2)}, u32[]{:S(2)}) collective-permute-start(bf16[32,1536]{1,0:T(8,128)(2,1)S(1)} %get-tuple-element.30), channel_id=1, source_target_pairs={{0,8},{2,10},{4,12},{6,14},{8,0},{10,2},{12,4},{14,6},{1,9},{3,11}... | collective-permute-start | bytes 294920 | tf_op jit(solution)/shard_map/ppermute | solution.py:248
  13.7 9.6 %collective-permute-start.10 = (bf16[32,1536]{1,0:T(8,128)(2,1)S(1)}, bf16[32,1536]{1,0:T(8,128)(2,1)S(1)}, u32[]{:S(2)}, u32[]{:S(2)}) collective-permute-start(bf16[32,1536]{1,0:T(8,128)(2,1)S(1)} %get-tuple-element.30), channel_id=1, source_target_pairs={{0,14},{2,12},{4,10},{6,8},{8,6},{10,4},{12,2},{14,0},{1,15},{3,13... | collective-permute-start | bytes 294920 | tf_op jit(solution)/shard_map/ppermute | solution.py:248
  14.8 8.5 %collective-permute-start.3 = (bf16[32,1536]{1,0:T(8,128)(2,1)S(1)}, bf16[32,1536]{1,0:T(8,128)(2,1)S(1)}, u32[]{:S(2)}, u32[]{:S(2)}) collective-permute-start(bf16[32,1536]{1,0:T(8,128)(2,1)S(1)} %collective-permute-done.2.refs_2_), channel_id=1, source_target_pairs={{0,2},{2,0},{4,6},{6,4},{8,10},{10,8},{12,14},{14,12},{1,3},{3,1},... | collective-permute-start | bytes 294920 | tf_op jit(solution)/shard_map/ppermute | solution.py:248
  21.3 4.6 %collective-permute-start.6 = (bf16[32,1536]{1,0:T(8,128)(2,1)S(1)}, bf16[32,1536]{1,0:T(8,128)(2,1)S(1)}, u32[]{:S(2)}, u32[]{:S(2)}) collective-permute-start(bf16[32,1536]{1,0:T(8,128)(2,1)S(1)} %collective-permute-done.5.refs_4_), channel_id=1, source_target_pairs={{0,2},{2,0},{4,6},{6,4},{8,10},{10,8},{12,14},{14,12},{1,3},{3,1},... | collective-permute-start | bytes 294920 | tf_op jit(solution)/shard_map/ppermute | solution.py:248
  23.3 4.6 %collective-permute-start.8 = (bf16[32,1536]{1,0:T(8,128)(2,1)S(1)}, bf16[32,1536]{1,0:T(8,128)(2,1)S(1)}, u32[]{:S(2)}, u32[]{:S(2)}) collective-permute-start(bf16[32,1536]{1,0:T(8,128)(2,1)S(1)} %collective-permute-done.5.refs_4_), channel_id=1, source_target_pairs={{0,4},{2,6},{4,0},{6,2},{8,12},{10,14},{12,8},{14,10},{1,5},{3,7},... | collective-permute-start | bytes 294920 | tf_op jit(solution)/shard_map/ppermute | solution.py:248
  23.3 4.6 %collective-permute-start.11 = (bf16[32,1536]{1,0:T(8,128)(2,1)S(1)}, bf16[32,1536]{1,0:T(8,128)(2,1)S(1)}, u32[]{:S(2)}, u32[]{:S(2)}) collective-permute-start(bf16[32,1536]{1,0:T(8,128)(2,1)S(1)} %collective-permute-done.10.refs_6_), channel_id=1, source_target_pairs={{0,1},{1,0},{2,3},{3,2},{4,5},{5,4},{6,7},{7,6},{8,9},{9,8},{10,11... | collective-permute-start | bytes 294920 | tf_op jit(solution)/shard_map/ppermute | solution.py:248
  23.3 4.6 %collective-permute-start.4 = (bf16[32,1536]{1,0:T(8,128)(2,1)S(1)}, bf16[32,1536]{1,0:T(8,128)(2,1)S(1)}, u32[]{:S(2)}, u32[]{:S(2)}) collective-permute-start(bf16[32,1536]{1,0:T(8,128)(2,1)S(1)} %collective-permute-done.3.refs_0_), channel_id=1, source_target_pairs={{0,1},{1,0},{2,3},{3,2},{4,5},{5,4},{6,7},{7,6},{8,9},{9,8},{10,11... | collective-permute-start | bytes 294920 | tf_op jit(solution)/shard_map/ppermute | solution.py:248
  25.9 2.0 %collective-permute-start.7 = (bf16[32,1536]{1,0:T(8,128)(2,1)S(1)}, bf16[32,1536]{1,0:T(8,128)(2,1)S(1)}, u32[]{:S(2)}, u32[]{:S(2)}) collective-permute-start(bf16[32,1536]{1,0:T(8,128)(2,1)S(1)} %collective-permute-done.6.refs_2_), channel_id=1, source_target_pairs={{0,1},{1,0},{2,3},{3,2},{4,5},{5,4},{6,7},{7,6},{8,9},{9,8},{10,11... | collective-permute-start | bytes 294920 | tf_op jit(solution)/shard_map/ppermute | solution.py:248
  27.9 1.3 %collective-permute-start.9 = (bf16[32,1536]{1,0:T(8,128)(2,1)S(1)}, bf16[32,1536]{1,0:T(8,128)(2,1)S(1)}, u32[]{:S(2)}, u32[]{:S(2)}) collective-permute-start(bf16[32,1536]{1,0:T(8,128)(2,1)S(1)} %collective-permute-done.8.refs_4_), channel_id=1, source_target_pairs={{0,1},{1,0},{2,3},{3,2},{4,5},{5,4},{6,7},{7,6},{8,9},{9,8},{10,11... | collective-permute-start | bytes 294920 | tf_op jit(solution)/shard_map/ppermute | solution.py:248
  31.5 9.1 %collective-permute-start.12 = (bf16[256,768]{1,0:T(8,128)(2,1)S(1)}, bf16[256,768]{1,0:T(8,128)(2,1)S(1)}, u32[]{:S(2)}, u32[]{:S(2)}) collective-permute-start(bf16[256,768]{1,0:T(8,128)(2,1)S(1)} %get-tuple-element.32), channel_id=1, source_target_pairs={{0,1},{1,0},{2,3},{3,2},{4,5},{5,4},{6,7},{7,6},{8,9},{9,8},{10,11... | collective-permute-start | bytes 1179656 | tf_op jit(solution)/shard_map/ppermute | solution.py:248
  31.7 5.1 %collective-permute-start.14 = (bf16[32,1536]{1,0:T(8,128)(2,1)S(1)}, bf16[32,1536]{1,0:T(8,128)(2,1)S(1)}, u32[]{:S(2)}, u32[]{:S(2)}) collective-permute-start(bf16[32,1536]{1,0:T(8,128)(2,1)S(1)} %get-tuple-element.30), channel_id=1, source_target_pairs={{0,2},{2,0},{4,6},{6,4},{8,10},{10,8},{12,14},{14,12},{1,3},{3,1},... | collective-permute-start | bytes 294920 | tf_op jit(solution)/shard_map/ppermute | solution.py:248
  36.8 1.3 %collective-permute-start.15 = (bf16[32,1536]{1,0:T(8,128)(2,1)S(1)}, bf16[32,1536]{1,0:T(8,128)(2,1)S(1)}, u32[]{:S(2)}, u32[]{:S(2)}) collective-permute-start(bf16[32,1536]{1,0:T(8,128)(2,1)S(1)} %collective-permute-done.14.refs_0_), channel_id=1, source_target_pairs={{0,1},{1,0},{2,3},{3,2},{4,5},{5,4},{6,7},{7,6},{8,9},{9,8},{10,11... | collective-permute-start | bytes 294920 | tf_op jit(solution)/shard_map/ppermute | solution.py:248
  36.8 1.5 %collective-permute-start.16 = (bf16[32,1536]{1,0:T(8,128)(2,1)S(1)}, bf16[32,1536]{1,0:T(8,128)(2,1)S(1)}, u32[]{:S(2)}, u32[]{:S(2)}) collective-permute-start(bf16[32,1536]{1,0:T(8,128)(2,1)S(1)} %collective-permute-done.2.refs_2_), channel_id=1, source_target_pairs={{0,1},{1,0},{2,3},{3,2},{4,5},{5,4},{6,7},{7,6},{8,9},{9,8},{10,11... | collective-permute-start | bytes 294920 | tf_op jit(solution)/shard_map/ppermute | solution.py:248
  37.3 1.3 %collective-permute-start.17 = (bf16[32,1536]{1,0:T(8,128)(2,1)S(1)}, bf16[32,1536]{1,0:T(8,128)(2,1)S(1)}, u32[]{:S(2)}, u32[]{:S(2)}) collective-permute-start(bf16[32,1536]{1,0:T(8,128)(2,1)S(1)} %collective-permute-done.5.refs_4_), channel_id=1, source_target_pairs={{0,1},{1,0},{2,3},{3,2},{4,5},{5,4},{6,7},{7,6},{8,9},{9,8},{10,11... | collective-permute-start | bytes 294920 | tf_op jit(solution)/shard_map/ppermute | solution.py:248
  40.4 3.9 %collective-permute-start.18 = (bf16[192,768]{1,0:T(8,128)(2,1)S(1)}, bf16[192,768]{1,0:T(8,128)(2,1)S(1)}, u32[]{:S(2)}, u32[]{:S(2)}) collective-permute-start(bf16[192,768]{1,0:T(8,128)(2,1)S(1)} %get-tuple-element.34), channel_id=1, source_target_pairs={{0,1},{1,0},{2,3},{3,2},{4,5},{5,4},{6,7},{7,6},{8,9},{9,8},{10,11... | collective-permute-start | bytes 884744 | tf_op jit(solution)/shard_map/ppermute | solution.py:248
  40.7 6.2 %collective-permute-start.20 = (bf16[64,768]{1,0:T(8,128)(2,1)S(1)}, bf16[64,768]{1,0:T(8,128)(2,1)S(1)}, u32[]{:S(2)}, u32[]{:S(2)}) collective-permute-start(bf16[64,768]{1,0:T(8,128)(2,1)S(1)} %get-tuple-element.37), channel_id=1, source_target_pairs={{0,2},{2,0},{4,6},{6,4},{8,10},{10,8},{12,14},{14,12},{1,3},{3,1},... | collective-permute-start | bytes 294920 | tf_op jit(solution)/shard_map/ppermute | solution.py:248
  41.1 5.9 %collective-permute-start.19 = (bf16[64,768]{1,0:T(8,128)(2,1)S(1)}, bf16[64,768]{1,0:T(8,128)(2,1)S(1)}, u32[]{:S(2)}, u32[]{:S(2)}) collective-permute-start(bf16[64,768]{1,0:T(8,128)(2,1)S(1)} %get-tuple-element.38), channel_id=1, source_target_pairs={{0,4},{2,6},{4,0},{6,2},{8,12},{10,14},{12,8},{14,10},{1,5},{3,7},... | collective-permute-start | bytes 294920 | tf_op jit(solution)/shard_map/ppermute | solution.py:248
  41.1 6.9 %collective-permute-start.22 = (bf16[64,768]{1,0:T(8,128)(2,1)S(1)}, bf16[64,768]{1,0:T(8,128)(2,1)S(1)}, u32[]{:S(2)}, u32[]{:S(2)}) collective-permute-start(bf16[64,768]{1,0:T(8,128)(2,1)S(1)} %get-tuple-element.36), channel_id=1, source_target_pairs={{0,2},{2,0},{4,6},{6,4},{8,10},{10,8},{12,14},{14,12},{1,3},{3,1},... | collective-permute-start | bytes 294920 | tf_op jit(solution)/shard_map/ppermute | solution.py:248
  44.3 7.5 %collective-permute-start.1 = (bf16[64,768]{1,0:T(8,128)(2,1)S(1)}, bf16[64,768]{1,0:T(8,128)(2,1)S(1)}, u32[]{:S(2)}, u32[]{:S(2)}) collective-permute-start(bf16[64,768]{1,0:T(8,128)(2,1)S(1)} %get-tuple-element.29), channel_id=1, source_target_pairs={{0,1},{1,0},{2,3},{3,2},{4,5},{5,4},{6,7},{7,6},{8,9},{9,8},{10,11... | collective-permute-start | bytes 294920 | tf_op jit(solution)/shard_map/ppermute | solution.py:248
  44.4 8.1 %collective-permute-start.13 = (bf16[64,768]{1,0:T(8,128)(2,1)S(1)}, bf16[64,768]{1,0:T(8,128)(2,1)S(1)}, u32[]{:S(2)}, u32[]{:S(2)}) collective-permute-start(bf16[64,768]{1,0:T(8,128)(2,1)S(1)} %get-tuple-element.35), channel_id=1, source_target_pairs={{0,14},{2,12},{4,10},{6,8},{8,6},{10,4},{12,2},{14,0},{1,15},{3,13... | collective-permute-start | bytes 294920 | tf_op jit(solution)/shard_map/ppermute | solution.py:248
  48.1 6.4 %collective-permute-start.24 = (bf16[64,768]{1,0:T(8,128)(2,1)S(1)}, bf16[64,768]{1,0:T(8,128)(2,1)S(1)}, u32[]{:S(2)}, u32[]{:S(2)}) collective-permute-start(bf16[64,768]{1,0:T(8,128)(2,1)S(1)} %get-tuple-element.40), channel_id=1, source_target_pairs={{0,2},{2,0},{4,6},{6,4},{8,10},{10,8},{12,14},{14,12},{1,3},{3,1},... | collective-permute-start | bytes 294920 | tf_op jit(solution)/shard_map/ppermute | solution.py:248
  48.6 5.8 %collective-permute-start.23 = (bf16[64,768]{1,0:T(8,128)(2,1)S(1)}, bf16[64,768]{1,0:T(8,128)(2,1)S(1)}, u32[]{:S(2)}, u32[]{:S(2)}) collective-permute-start(bf16[64,768]{1,0:T(8,128)(2,1)S(1)} %get-tuple-element.41), channel_id=1, source_target_pairs={{0,4},{2,6},{4,0},{6,2},{8,12},{10,14},{12,8},{14,10},{1,5},{3,7},... | collective-permute-start | bytes 294920 | tf_op jit(solution)/shard_map/ppermute | solution.py:248
  49.7 7.5 %collective-permute-start.21 = (bf16[64,768]{1,0:T(8,128)(2,1)S(1)}, bf16[64,768]{1,0:T(8,128)(2,1)S(1)}, u32[]{:S(2)}, u32[]{:S(2)}) collective-permute-start(bf16[64,768]{1,0:T(8,128)(2,1)S(1)} %get-tuple-element.39), channel_id=1, source_target_pairs={{0,8},{2,10},{4,12},{6,14},{8,0},{10,2},{12,4},{14,6},{1,9},{3,11}... | collective-permute-start | bytes 294920 | tf_op jit(solution)/shard_map/ppermute | solution.py:248

commit v2 on v1

--- a/solution.py
+++ b/solution.py
@@ -248,8 +248,9 @@
     return lax.ppermute(value, axis, [(i, i ^ offset) for i in range(lax.axis_size(axis))])
 
 
-def step_from(k, owners):
-    return 0 if k == owners - 1 else k & (k - 1)
+def step_from(k):
+    top = 1 << (k.bit_length() - 1)
+    return 0 if k == top else top
 
 
 def routed_all(stream, whole, mine, weights, experts):
@@ -258,8 +259,8 @@
     near = [k for k in range(1, owners) if k & (k - 1) == 0]
     far = [k for k in range(1, owners) if k not in near]
     half = {0: mine}
-    for k in sorted(near, reverse=True) + sorted(far, key=lambda k: (k.bit_count(), -k)):
-        source = step_from(k, owners)
+    for k in sorted(near, reverse=True) + far:
+        source = step_from(k)
         half[k] = flip(half[source], "ep", k ^ source)
     total = {}
     for name, group in (("own", [0]), ("near", near), ("far", far)):
@@ -273,8 +274,8 @@
         for i, k in enumerate(group):
             rows = slice(i * tokens, (i + 1) * tokens)
             total[k] = kept[rows] + received[rows].astype(jnp.float32)
-    for k in sorted(range(1, owners), key=lambda k: (-k.bit_count(), -k)):
-        target = step_from(k, owners)
+    for k in far + near:
+        target = step_from(k)
         part = flip(total[k].astype(jnp.bfloat16), "ep", k ^ target)
         total[target] = total[target] + part.astype(jnp.float32)
     return (stream + total[0][:, : stream.shape[1]]).astype(jnp.bfloat16)

time: 58.2 us -> 58.2 us (level)
  starting transfers between devices: 20.5 us -> 23.6 us
  waiting for transfers between devices: 24.4 us -> 21.5 us
    ppermute x25, starting transfers between devices: 20.5 us -> 23.6 us  [flip(): lax.ppermute(value, axis, [(i, i ^ offset) for i in range(lax.axis_size(a...]
    ppermute x25, waiting for transfers between devices: 24.4 us -> 21.5 us  [flip(): lax.ppermute(value, axis, [(i, i ^ offset) for i in range(lax.axis_size(a...]
  transfers between devices with their start and end apart: 25 -> 25, of which waited for: 13 -> 14; matrix products, arithmetic and copies ran while one was open for 0% -> 0% of each run, Pallas kernels for 6% -> 6%
where the time goes in v2:
time: 58.2 us; the launch traced here: 58.1 us
  starting transfers between devices  23.6 us (41%)
  waiting for transfers between devices  21.5 us (37%)
  Pallas kernels  12 us (21%)
  other arithmetic  0.89 us (2%)
    ppermute x25, starting transfers between devices, flip(): lax.ppermute(value, axis, [(i, i ^ offset) for i in range(lax.axis_size(a...  23.6 us
    ppermute x25, waiting for transfers between devices, flip(): lax.ppermute(value, axis, [(i, i ^ offset) for i in range(lax.axis_size(a...  21.5 us
    pallas_call x1, Pallas kernels, attend(): pl.pallas_call(functools.partial(attend_kernel, heads, experts), out_shap...  6.22 us
    pallas_call x3, Pallas kernels, expert(): pl.pallas_call(functools.partial(expert_kernel, experts, pieces), out_sha...  5.57 us
  transfers between devices with their start and end apart: 25, of which 14 were waited for; matrix products, arithmetic and copies ran while one was open for 0% of the time, Pallas kernels for 6%

profile of v2, /device:TPU:0, one launch (start us, length us, event | category | flops | bytes accessed | tf_op | source)
XLA Modules:
  0.0 58.1 jit_solution(16674614119825682116)
XLA Ops:
  0.0 6.2 %attend.1 = (f32[64,1440]{1,0:T(8,128)S(1)}, bf16[64,1440]{1,0:T(8,128)(2,1)S(1)}, bf16[64,16]{1,0:T(8,128)(2,1)S(1)}, bf16[1440,720]{1,0:T(8,128)(2,1)S(1)}, bf...) custom-call(s32[12,64]{1,0:T(8,128)} %bitcast.11, s32[64]{0:T(128)} %length_in.1, bf16[64,1024]{1,0:T(8,128)(2,1)} %q_in.1, ...), custom_call_target="tpu_custom_call" | custom-call | tf_op jit(solution)/shard_map/attend/pallas_call | solution.py:136
  6.2 0.6 collective-permute-start
  6.8 1.1 %collective-permute-done.other = bf16[64,1440]{1,0:T(8,128)(2,1)S(1)} collective-permute-done((bf16[64,1440]{1,0:T(8,128)(2,1)S(1)}, bf16[64,1440]{1,0:T(8,128)(2,1)S(1)}, u32[]{:S(2)}, u32[]{:S(2)}) %collective-permute-start) | collective-permute-done | bytes 184352 | tf_op jit(solution)/shard_map/ppermute | solution.py:248
  7.9 0.2 norm.1
  8.1 4.0 %collective-permute-start.6 = (bf16[32,1536]{1,0:T(8,128)(2,1)S(1)}, bf16[32,1536]{1,0:T(8,128)(2,1)S(1)}, u32[]{:S(2)}, u32[]{:S(2)}) collective-permute-start(bf16[32,1536]{1,0:T(8,128)(2,1)S(1)} %get-tuple-element.30), channel_id=1, source_target_pairs={{0,8},{2,10},{4,12},{6,14},{8,0},{10,2},{12,4},{14,6},{1,9},{3,11}... | collective-permute-start | bytes 294920 | tf_op jit(solution)/shard_map/ppermute | solution.py:248
  12.1 1.6 %collective-permute-start.4 = (bf16[32,1536]{1,0:T(8,128)(2,1)S(1)}, bf16[32,1536]{1,0:T(8,128)(2,1)S(1)}, u32[]{:S(2)}, u32[]{:S(2)}) collective-permute-start(bf16[32,1536]{1,0:T(8,128)(2,1)S(1)} %get-tuple-element.30), channel_id=1, source_target_pairs={{0,4},{2,6},{4,0},{6,2},{8,12},{10,14},{12,8},{14,10},{1,5},{3,7},... | collective-permute-start | bytes 294920 | tf_op jit(solution)/shard_map/ppermute | solution.py:248
  13.7 3.7 %collective-permute-done.6.refs_4_ = bf16[32,1536]{1,0:T(8,128)(2,1)S(1)} collective-permute-done((bf16[32,1536]{1,0:T(8,128)(2,1)S(1)}, bf16[32,1536]{1,0:T(8,128)(2,1)S(1)}, u32[]{:S(2)}, u32[]{:S(2)}) %collective-permute-start.6) | collective-permute-done | bytes 98336 | tf_op jit(solution)/shard_map/ppermute | solution.py:248
  17.4 1.5 %collective-permute-start.12 = (bf16[32,1536]{1,0:T(8,128)(2,1)S(1)}, bf16[32,1536]{1,0:T(8,128)(2,1)S(1)}, u32[]{:S(2)}, u32[]{:S(2)}) collective-permute-start(bf16[32,1536]{1,0:T(8,128)(2,1)S(1)} %collective-permute-done.6.refs_4_), channel_id=1, source_target_pairs={{0,2},{2,0},{4,6},{6,4},{8,10},{10,8},{12,14},{14,12},{1,3},{3,1},... | collective-permute-start | bytes 294920 | tf_op jit(solution)/shard_map/ppermute | solution.py:248
  19.0 0.6 collective-permute-start.14
  19.5 1.4 %collective-permute-start.16 = (bf16[32,1536]{1,0:T(8,128)(2,1)S(1)}, bf16[32,1536]{1,0:T(8,128)(2,1)S(1)}, u32[]{:S(2)}, u32[]{:S(2)}) collective-permute-start(bf16[32,1536]{1,0:T(8,128)(2,1)S(1)} %collective-permute-done.6.refs_4_), channel_id=1, source_target_pairs={{0,6},{2,4},{4,2},{6,0},{8,14},{10,12},{12,10},{14,8},{1,7},{3,5},... | collective-permute-start | bytes 294920 | tf_op jit(solution)/shard_map/ppermute | solution.py:248
  20.9 1.5 %collective-permute-start.10 = (bf16[32,1536]{1,0:T(8,128)(2,1)S(1)}, bf16[32,1536]{1,0:T(8,128)(2,1)S(1)}, u32[]{:S(2)}, u32[]{:S(2)}) collective-permute-start(bf16[32,1536]{1,0:T(8,128)(2,1)S(1)} %collective-permute-done.4.refs_2_), channel_id=1, source_target_pairs={{0,2},{2,0},{4,6},{6,4},{8,10},{10,8},{12,14},{14,12},{1,3},{3,1},... | collective-permute-start | bytes 294920 | tf_op jit(solution)/shard_map/ppermute | solution.py:248
  22.5 0.2 collective-permute-done.12.refs_2_
  22.7 1.0 %collective-permute-done.14.refs_4_ = bf16[32,1536]{1,0:T(8,128)(2,1)S(1)} collective-permute-done((bf16[32,1536]{1,0:T(8,128)(2,1)S(1)}, bf16[32,1536]{1,0:T(8,128)(2,1)S(1)}, u32[]{:S(2)}, u32[]{:S(2)}) %collective-permute-start.14) | collective-permute-done | bytes 98336 | tf_op jit(solution)/shard_map/ppermute | solution.py:248
  23.7 2.0 %collective-permute-done.16.refs_6_ = bf16[32,1536]{1,0:T(8,128)(2,1)S(1)} collective-permute-done((bf16[32,1536]{1,0:T(8,128)(2,1)S(1)}, bf16[32,1536]{1,0:T(8,128)(2,1)S(1)}, u32[]{:S(2)}, u32[]{:S(2)}) %collective-permute-start.16) | collective-permute-done | bytes 98336 | tf_op jit(solution)/shard_map/ppermute | solution.py:248
  25.7 0.0 collective-permute-start.17
  25.7 0.9 %collective-permute-done.10.refs_0_ = bf16[32,1536]{1,0:T(8,128)(2,1)S(1)} collective-permute-done((bf16[32,1536]{1,0:T(8,128)(2,1)S(1)}, bf16[32,1536]{1,0:T(8,128)(2,1)S(1)}, u32[]{:S(2)}, u32[]{:S(2)}) %collective-permute-start.10) | collective-permute-done | bytes 98336 | tf_op jit(solution)/shard_map/ppermute | solution.py:248
  26.7 0.0 collective-permute-start.11
  26.7 0.0 collective-permute-done.13.refs_3_
  26.7 0.0 collective-permute-done.15.refs_5_
  26.7 0.3 collective-permute-done.17.refs_7_
  27.0 0.9 %collective-permute-done.11.refs_1_ = bf16[32,1536]{1,0:T(8,128)(2,1)S(1)} collective-permute-done((bf16[32,1536]{1,0:T(8,128)(2,1)S(1)}, bf16[32,1536]{1,0:T(8,128)(2,1)S(1)}, u32[]{:S(2)}, u32[]{:S(2)}) %collective-permute-start.11) | collective-permute-done | bytes 98336 | tf_op jit(solution)/shard_map/ppermute | solution.py:248
  28.0 2.3 %expert.5 = (f32[256,768]{1,0:T(8,128)S(1)}, bf16[256,768]{1,0:T(8,128)(2,1)S(1)}) custom-call(bf16[32,1536]{1,0:T(8,128)(2,1)S(1)} %collective-permute-done.10.refs_0_, bf16[32,1536]{1,0:T(8,128)(2,1)S(1)} %collective-permute-done.11.refs_1_, bf16[32,1536]{1,0:T(8,128)(2,1)S(1)} %collective-permute-done.12.refs_2_, ...), custom_call_target="tpu_custom_call" | custom-call | flops 1592524800 | bytes 6220800 | tf_op jit(solution)/shard_map/expert/pallas_call | solution.py:230
  30.3 0.2 collective-permute-start.18
  30.5 1.1 %collective-permute-start.2 = (bf16[32,1536]{1,0:T(8,128)(2,1)S(1)}, bf16[32,1536]{1,0:T(8,128)(2,1)S(1)}, u32[]{:S(2)}, u32[]{:S(2)}) collective-permute-start(bf16[32,1536]{1,0:T(8,128)(2,1)S(1)} %get-tuple-element.30), channel_id=1, source_target_pairs={{0,2},{2,0},{4,6},{6,4},{8,10},{10,8},{12,14},{14,12},{1,3},{3,1},... | collective-permute-start | bytes 294920 | tf_op jit(solution)/shard_map/ppermute | solution.py:248
  31.6 0.1 collective-permute-start.7
  31.7 0.4 collective-permute-start.5
  32.1 3.4 %collective-permute-done.2.refs_0_ = bf16[32,1536]{1,0:T(8,128)(2,1)S(1)} collective-permute-done((bf16[32,1536]{1,0:T(8,128)(2,1)S(1)}, bf16[32,1536]{1,0:T(8,128)(2,1)S(1)}, u32[]{:S(2)}, u32[]{:S(2)}) %collective-permute-start.2) | collective-permute-done | bytes 98336 | tf_op jit(solution)/shard_map/ppermute | solution.py:248
  35.5 1.3 %collective-permute-done.3.refs_1_ = bf16[32,1536]{1,0:T(8,128)(2,1)S(1)} collective-permute-done((bf16[32,1536]{1,0:T(8,128)(2,1)S(1)}, bf16[32,1536]{1,0:T(8,128)(2,1)S(1)}, u32[]{:S(2)}, u32[]{:S(2)}) %collective-permute-start.3) | collective-permute-done | bytes 98336 | tf_op jit(solution)/shard_map/ppermute | solution.py:248
  36.8 1.8 %expert.4 = (f32[192,768]{1,0:T(8,128)S(1)}, bf16[192,768]{1,0:T(8,128)(2,1)S(1)}) custom-call(bf16[32,1536]{1,0:T(8,128)(2,1)S(1)} %collective-permute-done.2.refs_0_, bf16[32,1536]{1,0:T(8,128)(2,1)S(1)} %collective-permute-done.3.refs_1_, bf16[32,1536]{1,0:T(8,128)(2,1)S(1)} %collective-permute-done.4.refs_2_, ...), custom_call_target="tpu_custom_call" | custom-call | flops 1194393600 | bytes 6220800 | tf_op jit(solution)/shard_map/expert/pallas_call | solution.py:230
  38.7 0.2 collective-permute-start.8
  38.9 0.1 add_convert_fusion.5
  39.0 1.2 %collective-permute-start.19 = (bf16[64,768]{1,0:T(8,128)(2,1)S(1)}, bf16[64,768]{1,0:T(8,128)(2,1)S(1)}, u32[]{:S(2)}, u32[]{:S(2)}) collective-permute-start(bf16[64,768]{1,0:T(8,128)(2,1)S(1)} %get-tuple-element.35), channel_id=1, source_target_pairs={{0,2},{2,0},{4,6},{6,4},{8,10},{10,8},{12,14},{14,12},{1,3},{3,1},... | collective-permute-start | bytes 294920 | tf_op jit(solution)/shard_map/ppermute | solution.py:248
  40.2 0.9 %collective-permute-start.21 = (bf16[64,768]{1,0:T(8,128)(2,1)S(1)}, bf16[64,768]{1,0:T(8,128)(2,1)S(1)}, u32[]{:S(2)}, u32[]{:S(2)}) collective-permute-start(bf16[64,768]{1,0:T(8,128)(2,1)S(1)} %get-tuple-element.38), channel_id=1, source_target_pairs={{0,2},{2,0},{4,6},{6,4},{8,10},{10,8},{12,14},{14,12},{1,3},{3,1},... | collective-permute-start | bytes 294920 | tf_op jit(solution)/shard_map/ppermute | solution.py:248
  41.1 0.6 %collective-permute-start.22 = (bf16[64,768]{1,0:T(8,128)(2,1)S(1)}, bf16[64,768]{1,0:T(8,128)(2,1)S(1)}, u32[]{:S(2)}, u32[]{:S(2)}) collective-permute-start(bf16[64,768]{1,0:T(8,128)(2,1)S(1)} %get-tuple-element.37), channel_id=1, source_target_pairs={{0,4},{2,6},{4,0},{6,2},{8,12},{10,14},{12,8},{14,10},{1,5},{3,7},... | collective-permute-start | bytes 294920 | tf_op jit(solution)/shard_map/ppermute | solution.py:248
  41.6 2.0 %collective-permute-start.23 = (bf16[64,768]{1,0:T(8,128)(2,1)S(1)}, bf16[64,768]{1,0:T(8,128)(2,1)S(1)}, u32[]{:S(2)}, u32[]{:S(2)}) collective-permute-start(bf16[64,768]{1,0:T(8,128)(2,1)S(1)} %get-tuple-element.36), channel_id=1, source_target_pairs={{0,6},{2,4},{4,2},{6,0},{8,14},{10,12},{12,10},{14,8},{1,7},{3,5},... | collective-permute-start | bytes 294920 | tf_op jit(solution)/shard_map/ppermute | solution.py:248
  43.7 1.4 %expert.3 = (f32[64,768]{1,0:T(8,128)S(1)}, bf16[64,768]{1,0:T(8,128)(2,1)S(1)}) custom-call(bf16[64,1536]{1,0:T(8,128)(2,1)S(1)} %get-tuple-element.24.refs_0_, bf16[1440,720]{1,0:T(8,128)(2,1)S(1)} %get-tuple-element.25.refs_1_.refs_6_.refs_8_, bf16[1440,720]{1,0:T(8,128)(2,1)S(1)} %get-tuple-element.26.refs_2_.refs_7_.refs_9_, ...), custom_call_target="tpu_custom_call" | custom-call | flops 398131200 | bytes 6220800 | tf_op jit(solution)/shard_map/expert/pallas_call | solution.py:230
  45.1 0.1 collective-permute-start.1
  45.2 0.0 collective-permute-done.19
  45.2 3.1 %collective-permute-done.21 = bf16[64,768]{1,0:T(8,128)(2,1)S(1)} collective-permute-done((bf16[64,768]{1,0:T(8,128)(2,1)S(1)}, bf16[64,768]{1,0:T(8,128)(2,1)S(1)}, u32[]{:S(2)}, u32[]{:S(2)}) %collective-permute-start.21) | collective-permute-done | bytes 98336 | tf_op jit(solution)/shard_map/ppermute | solution.py:248
  48.3 0.0 collective-permute-done.23
  48.3 0.1 add_convert_fusion.6
  48.4 1.0 %collective-permute-start.20 = (bf16[64,768]{1,0:T(8,128)(2,1)S(1)}, bf16[64,768]{1,0:T(8,128)(2,1)S(1)}, u32[]{:S(2)}, u32[]{:S(2)}) collective-permute-start(bf16[64,768]{1,0:T(8,128)(2,1)S(1)} %get-tuple-element.41), channel_id=1, source_target_pairs={{0,4},{2,6},{4,0},{6,2},{8,12},{10,14},{12,8},{14,10},{1,5},{3,7},... | collective-permute-start | bytes 294920 | tf_op jit(solution)/shard_map/ppermute | solution.py:248
  49.4 3.3 %collective-permute-start.24 = (bf16[64,768]{1,0:T(8,128)(2,1)S(1)}, bf16[64,768]{1,0:T(8,128)(2,1)S(1)}, u32[]{:S(2)}, u32[]{:S(2)}) collective-permute-start(bf16[64,768]{1,0:T(8,128)(2,1)S(1)} %get-tuple-element.40), channel_id=1, source_target_pairs={{0,8},{2,10},{4,12},{6,14},{8,0},{10,2},{12,4},{14,6},{1,9},{3,11}... | collective-permute-start | bytes 294920 | tf_op jit(solution)/shard_map/ppermute | solution.py:248
  52.7 1.2 %collective-permute-start.9 = (bf16[64,768]{1,0:T(8,128)(2,1)S(1)}, bf16[64,768]{1,0:T(8,128)(2,1)S(1)}, u32[]{:S(2)}, u32[]{:S(2)}) collective-permute-start(bf16[64,768]{1,0:T(8,128)(2,1)S(1)} %get-tuple-element.39), channel_id=1, source_target_pairs={{0,2},{2,0},{4,6},{6,4},{8,10},{10,8},{12,14},{14,12},{1,3},{3,1},... | collective-permute-start | bytes 294920 | tf_op jit(solution)/shard_map/ppermute | solution.py:248
  53.9 0.1 collective-permute-done.20
  54.0 1.3 %collective-permute-done.24 = bf16[64,768]{1,0:T(8,128)(2,1)S(1)} collective-permute-done((bf16[64,768]{1,0:T(8,128)(2,1)S(1)}, bf16[64,768]{1,0:T(8,128)(2,1)S(1)}, u32[]{:S(2)}, u32[]{:S(2)}) %collective-permute-start.24) | collective-permute-done | bytes 98336 | tf_op jit(solution)/shard_map/ppermute | solution.py:248
  55.3 2.0 %collective-permute-done.9 = bf16[64,768]{1,0:T(8,128)(2,1)S(1)} collective-permute-done((bf16[64,768]{1,0:T(8,128)(2,1)S(1)}, bf16[64,768]{1,0:T(8,128)(2,1)S(1)}, u32[]{:S(2)}, u32[]{:S(2)}) %collective-permute-start.9) | collective-permute-done | bytes 98336 | tf_op jit(solution)/shard_map/ppermute | solution.py:248
  57.3 0.7 %fusion.4 = bf16[64,720]{1,0:T(8,128)(2,1)} fusion(f32[64,720]{1,0:T(8,128)S(1)} %get-tuple-element.23, f32[64,768]{1,0:T(8,128)S(1)} %get-tuple-element.28, bf16[64,768]{1,0:T(8,128)(2,1)S(1)} %collective-permute-done.24, bf16[64,768]{1,0:T(8,128)(2,1)S(1)} %collective-permute-done.20, bf16[64,768]{1,0:T(8,128)(2,1)S(1)} %collective-permute-done.9, ...), kind=kLoop, calls=%fused_computation.5 | loop fusion | flops 460800 | bytes 829440 | tf_op jit(solution)/shard_map/convert_element_type | solution.py:281
  (15 shorter events, 0.0 us)
Async XLA Ops:
  0.0 6.8 %copy-start.1 = (f32[1440]{0:T(1024)S(1)}, f32[1440]{0:T(1024)}, u32[]{:S(2)}) copy-start(f32[1440]{0:T(1024)} %param.19) | copy-start | bytes 17284
  0.0 7.9 %copy-start = (bf16[64,1440]{1,0:T(8,128)(2,1)S(1)}, bf16[64,1440]{1,0:T(8,128)(2,1)}, u32[]{:S(2)}) copy-start(bf16[64,1440]{1,0:T(8,128)(2,1)} %resid.1) | copy-start | bytes 552964
  6.2 1.6 %collective-permute-start = (bf16[64,1440]{1,0:T(8,128)(2,1)S(1)}, bf16[64,1440]{1,0:T(8,128)(2,1)S(1)}, u32[]{:S(2)}, u32[]{:S(2)}) collective-permute-start(bf16[64,1440]{1,0:T(8,128)(2,1)S(1)} %get-tuple-element.21), channel_id=1, source_target_pairs={{0,1},{1,0},{2,3},{3,2},{4,5},{5,4},{6,7},{7,6},{8,9},{9,8},{10,11... | collective-permute-start | bytes 552968 | tf_op jit(solution)/shard_map/ppermute | solution.py:248
  8.1 9.3 %collective-permute-start.6 = (bf16[32,1536]{1,0:T(8,128)(2,1)S(1)}, bf16[32,1536]{1,0:T(8,128)(2,1)S(1)}, u32[]{:S(2)}, u32[]{:S(2)}) collective-permute-start(bf16[32,1536]{1,0:T(8,128)(2,1)S(1)} %get-tuple-element.30), channel_id=1, source_target_pairs={{0,8},{2,10},{4,12},{6,14},{8,0},{10,2},{12,4},{14,6},{1,9},{3,11}... | collective-permute-start | bytes 294920 | tf_op jit(solution)/shard_map/ppermute | solution.py:248
  12.1 8.8 %collective-permute-start.4 = (bf16[32,1536]{1,0:T(8,128)(2,1)S(1)}, bf16[32,1536]{1,0:T(8,128)(2,1)S(1)}, u32[]{:S(2)}, u32[]{:S(2)}) collective-permute-start(bf16[32,1536]{1,0:T(8,128)(2,1)S(1)} %get-tuple-element.30), channel_id=1, source_target_pairs={{0,4},{2,6},{4,0},{6,2},{8,12},{10,14},{12,8},{14,10},{1,5},{3,7},... | collective-permute-start | bytes 294920 | tf_op jit(solution)/shard_map/ppermute | solution.py:248
  17.4 5.2 %collective-permute-start.12 = (bf16[32,1536]{1,0:T(8,128)(2,1)S(1)}, bf16[32,1536]{1,0:T(8,128)(2,1)S(1)}, u32[]{:S(2)}, u32[]{:S(2)}) collective-permute-start(bf16[32,1536]{1,0:T(8,128)(2,1)S(1)} %collective-permute-done.6.refs_4_), channel_id=1, source_target_pairs={{0,2},{2,0},{4,6},{6,4},{8,10},{10,8},{12,14},{14,12},{1,3},{3,1},... | collective-permute-start | bytes 294920 | tf_op jit(solution)/shard_map/ppermute | solution.py:248
  19.0 4.7 %collective-permute-start.14 = (bf16[32,1536]{1,0:T(8,128)(2,1)S(1)}, bf16[32,1536]{1,0:T(8,128)(2,1)S(1)}, u32[]{:S(2)}, u32[]{:S(2)}) collective-permute-start(bf16[32,1536]{1,0:T(8,128)(2,1)S(1)} %collective-permute-done.6.refs_4_), channel_id=1, source_target_pairs={{0,4},{2,6},{4,0},{6,2},{8,12},{10,14},{12,8},{14,10},{1,5},{3,7},... | collective-permute-start | bytes 294920 | tf_op jit(solution)/shard_map/ppermute | solution.py:248
  19.5 6.2 %collective-permute-start.16 = (bf16[32,1536]{1,0:T(8,128)(2,1)S(1)}, bf16[32,1536]{1,0:T(8,128)(2,1)S(1)}, u32[]{:S(2)}, u32[]{:S(2)}) collective-permute-start(bf16[32,1536]{1,0:T(8,128)(2,1)S(1)} %collective-permute-done.6.refs_4_), channel_id=1, source_target_pairs={{0,6},{2,4},{4,2},{6,0},{8,14},{10,12},{12,10},{14,8},{1,7},{3,5},... | collective-permute-start | bytes 294920 | tf_op jit(solution)/shard_map/ppermute | solution.py:248
  20.9 5.7 %collective-permute-start.10 = (bf16[32,1536]{1,0:T(8,128)(2,1)S(1)}, bf16[32,1536]{1,0:T(8,128)(2,1)S(1)}, u32[]{:S(2)}, u32[]{:S(2)}) collective-permute-start(bf16[32,1536]{1,0:T(8,128)(2,1)S(1)} %collective-permute-done.4.refs_2_), channel_id=1, source_target_pairs={{0,2},{2,0},{4,6},{6,4},{8,10},{10,8},{12,14},{14,12},{1,3},{3,1},... | collective-permute-start | bytes 294920 | tf_op jit(solution)/shard_map/ppermute | solution.py:248
  22.7 4.0 %collective-permute-start.13 = (bf16[32,1536]{1,0:T(8,128)(2,1)S(1)}, bf16[32,1536]{1,0:T(8,128)(2,1)S(1)}, u32[]{:S(2)}, u32[]{:S(2)}) collective-permute-start(bf16[32,1536]{1,0:T(8,128)(2,1)S(1)} %collective-permute-done.12.refs_2_), channel_id=1, source_target_pairs={{0,1},{1,0},{2,3},{3,2},{4,5},{5,4},{6,7},{7,6},{8,9},{9,8},{10,11... | collective-permute-start | bytes 294920 | tf_op jit(solution)/shard_map/ppermute | solution.py:248
  23.7 3.0 %collective-permute-start.15 = (bf16[32,1536]{1,0:T(8,128)(2,1)S(1)}, bf16[32,1536]{1,0:T(8,128)(2,1)S(1)}, u32[]{:S(2)}, u32[]{:S(2)}) collective-permute-start(bf16[32,1536]{1,0:T(8,128)(2,1)S(1)} %collective-permute-done.14.refs_4_), channel_id=1, source_target_pairs={{0,1},{1,0},{2,3},{3,2},{4,5},{5,4},{6,7},{7,6},{8,9},{9,8},{10,11... | collective-permute-start | bytes 294920 | tf_op jit(solution)/shard_map/ppermute | solution.py:248
  25.7 1.3 %collective-permute-start.17 = (bf16[32,1536]{1,0:T(8,128)(2,1)S(1)}, bf16[32,1536]{1,0:T(8,128)(2,1)S(1)}, u32[]{:S(2)}, u32[]{:S(2)}) collective-permute-start(bf16[32,1536]{1,0:T(8,128)(2,1)S(1)} %collective-permute-done.16.refs_6_), channel_id=1, source_target_pairs={{0,1},{1,0},{2,3},{3,2},{4,5},{5,4},{6,7},{7,6},{8,9},{9,8},{10,11... | collective-permute-start | bytes 294920 | tf_op jit(solution)/shard_map/ppermute | solution.py:248
  26.7 1.3 %collective-permute-start.11 = (bf16[32,1536]{1,0:T(8,128)(2,1)S(1)}, bf16[32,1536]{1,0:T(8,128)(2,1)S(1)}, u32[]{:S(2)}, u32[]{:S(2)}) collective-permute-start(bf16[32,1536]{1,0:T(8,128)(2,1)S(1)} %collective-permute-done.10.refs_0_), channel_id=1, source_target_pairs={{0,1},{1,0},{2,3},{3,2},{4,5},{5,4},{6,7},{7,6},{8,9},{9,8},{10,11... | collective-permute-start | bytes 294920 | tf_op jit(solution)/shard_map/ppermute | solution.py:248
  30.3 8.6 %collective-permute-start.18 = (bf16[256,768]{1,0:T(8,128)(2,1)S(1)}, bf16[256,768]{1,0:T(8,128)(2,1)S(1)}, u32[]{:S(2)}, u32[]{:S(2)}) collective-permute-start(bf16[256,768]{1,0:T(8,128)(2,1)S(1)} %get-tuple-element.34), channel_id=1, source_target_pairs={{0,1},{1,0},{2,3},{3,2},{4,5},{5,4},{6,7},{7,6},{8,9},{9,8},{10,11... | collective-permute-start | bytes 1179656 | tf_op jit(solution)/shard_map/ppermute | solution.py:248
  30.5 5.1 %collective-permute-start.2 = (bf16[32,1536]{1,0:T(8,128)(2,1)S(1)}, bf16[32,1536]{1,0:T(8,128)(2,1)S(1)}, u32[]{:S(2)}, u32[]{:S(2)}) collective-permute-start(bf16[32,1536]{1,0:T(8,128)(2,1)S(1)} %get-tuple-element.30), channel_id=1, source_target_pairs={{0,2},{2,0},{4,6},{6,4},{8,10},{10,8},{12,14},{14,12},{1,3},{3,1},... | collective-permute-start | bytes 294920 | tf_op jit(solution)/shard_map/ppermute | solution.py:248
  31.6 3.9 %collective-permute-start.7 = (bf16[32,1536]{1,0:T(8,128)(2,1)S(1)}, bf16[32,1536]{1,0:T(8,128)(2,1)S(1)}, u32[]{:S(2)}, u32[]{:S(2)}) collective-permute-start(bf16[32,1536]{1,0:T(8,128)(2,1)S(1)} %collective-permute-done.6.refs_4_), channel_id=1, source_target_pairs={{0,1},{1,0},{2,3},{3,2},{4,5},{5,4},{6,7},{7,6},{8,9},{9,8},{10,11... | collective-permute-start | bytes 294920 | tf_op jit(solution)/shard_map/ppermute | solution.py:248
  31.7 3.8 %collective-permute-start.5 = (bf16[32,1536]{1,0:T(8,128)(2,1)S(1)}, bf16[32,1536]{1,0:T(8,128)(2,1)S(1)}, u32[]{:S(2)}, u32[]{:S(2)}) collective-permute-start(bf16[32,1536]{1,0:T(8,128)(2,1)S(1)} %collective-permute-done.4.refs_2_), channel_id=1, source_target_pairs={{0,1},{1,0},{2,3},{3,2},{4,5},{5,4},{6,7},{7,6},{8,9},{9,8},{10,11... | collective-permute-start | bytes 294920 | tf_op jit(solution)/shard_map/ppermute | solution.py:248
  35.5 1.3 %collective-permute-start.3 = (bf16[32,1536]{1,0:T(8,128)(2,1)S(1)}, bf16[32,1536]{1,0:T(8,128)(2,1)S(1)}, u32[]{:S(2)}, u32[]{:S(2)}) collective-permute-start(bf16[32,1536]{1,0:T(8,128)(2,1)S(1)} %collective-permute-done.2.refs_0_), channel_id=1, source_target_pairs={{0,1},{1,0},{2,3},{3,2},{4,5},{5,4},{6,7},{7,6},{8,9},{9,8},{10,11... | collective-permute-start | bytes 294920 | tf_op jit(solution)/shard_map/ppermute | solution.py:248
  38.7 6.4 %collective-permute-start.8 = (bf16[192,768]{1,0:T(8,128)(2,1)S(1)}, bf16[192,768]{1,0:T(8,128)(2,1)S(1)}, u32[]{:S(2)}, u32[]{:S(2)}) collective-permute-start(bf16[192,768]{1,0:T(8,128)(2,1)S(1)} %get-tuple-element.32), channel_id=1, source_target_pairs={{0,1},{1,0},{2,3},{3,2},{4,5},{5,4},{6,7},{7,6},{8,9},{9,8},{10,11... | collective-permute-start | bytes 884744 | tf_op jit(solution)/shard_map/ppermute | solution.py:248
  39.0 6.2 %collective-permute-start.19 = (bf16[64,768]{1,0:T(8,128)(2,1)S(1)}, bf16[64,768]{1,0:T(8,128)(2,1)S(1)}, u32[]{:S(2)}, u32[]{:S(2)}) collective-permute-start(bf16[64,768]{1,0:T(8,128)(2,1)S(1)} %get-tuple-element.35), channel_id=1, source_target_pairs={{0,2},{2,0},{4,6},{6,4},{8,10},{10,8},{12,14},{14,12},{1,3},{3,1},... | collective-permute-start | bytes 294920 | tf_op jit(solution)/shard_map/ppermute | solution.py:248
  40.2 8.1 %collective-permute-start.21 = (bf16[64,768]{1,0:T(8,128)(2,1)S(1)}, bf16[64,768]{1,0:T(8,128)(2,1)S(1)}, u32[]{:S(2)}, u32[]{:S(2)}) collective-permute-start(bf16[64,768]{1,0:T(8,128)(2,1)S(1)} %get-tuple-element.38), channel_id=1, source_target_pairs={{0,2},{2,0},{4,6},{6,4},{8,10},{10,8},{12,14},{14,12},{1,3},{3,1},... | collective-permute-start | bytes 294920 | tf_op jit(solution)/shard_map/ppermute | solution.py:248
  41.1 7.2 %collective-permute-start.22 = (bf16[64,768]{1,0:T(8,128)(2,1)S(1)}, bf16[64,768]{1,0:T(8,128)(2,1)S(1)}, u32[]{:S(2)}, u32[]{:S(2)}) collective-permute-start(bf16[64,768]{1,0:T(8,128)(2,1)S(1)} %get-tuple-element.37), channel_id=1, source_target_pairs={{0,4},{2,6},{4,0},{6,2},{8,12},{10,14},{12,8},{14,10},{1,5},{3,7},... | collective-permute-start | bytes 294920 | tf_op jit(solution)/shard_map/ppermute | solution.py:248
  41.6 6.7 %collective-permute-start.23 = (bf16[64,768]{1,0:T(8,128)(2,1)S(1)}, bf16[64,768]{1,0:T(8,128)(2,1)S(1)}, u32[]{:S(2)}, u32[]{:S(2)}) collective-permute-start(bf16[64,768]{1,0:T(8,128)(2,1)S(1)} %get-tuple-element.36), channel_id=1, source_target_pairs={{0,6},{2,4},{4,2},{6,0},{8,14},{10,12},{12,10},{14,8},{1,7},{3,5},... | collective-permute-start | bytes 294920 | tf_op jit(solution)/shard_map/ppermute | solution.py:248
  45.1 8.8 %collective-permute-start.1 = (bf16[64,768]{1,0:T(8,128)(2,1)S(1)}, bf16[64,768]{1,0:T(8,128)(2,1)S(1)}, u32[]{:S(2)}, u32[]{:S(2)}) collective-permute-start(bf16[64,768]{1,0:T(8,128)(2,1)S(1)} %get-tuple-element.29), channel_id=1, source_target_pairs={{0,1},{1,0},{2,3},{3,2},{4,5},{5,4},{6,7},{7,6},{8,9},{9,8},{10,11... | collective-permute-start | bytes 294920 | tf_op jit(solution)/shard_map/ppermute | solution.py:248
  48.4 5.6 %collective-permute-start.20 = (bf16[64,768]{1,0:T(8,128)(2,1)S(1)}, bf16[64,768]{1,0:T(8,128)(2,1)S(1)}, u32[]{:S(2)}, u32[]{:S(2)}) collective-permute-start(bf16[64,768]{1,0:T(8,128)(2,1)S(1)} %get-tuple-element.41), channel_id=1, source_target_pairs={{0,4},{2,6},{4,0},{6,2},{8,12},{10,14},{12,8},{14,10},{1,5},{3,7},... | collective-permute-start | bytes 294920 | tf_op jit(solution)/shard_map/ppermute | solution.py:248
  49.4 5.9 %collective-permute-start.24 = (bf16[64,768]{1,0:T(8,128)(2,1)S(1)}, bf16[64,768]{1,0:T(8,128)(2,1)S(1)}, u32[]{:S(2)}, u32[]{:S(2)}) collective-permute-start(bf16[64,768]{1,0:T(8,128)(2,1)S(1)} %get-tuple-element.40), channel_id=1, source_target_pairs={{0,8},{2,10},{4,12},{6,14},{8,0},{10,2},{12,4},{14,6},{1,9},{3,11}... | collective-permute-start | bytes 294920 | tf_op jit(solution)/shard_map/ppermute | solution.py:248
  52.7 4.6 %collective-permute-start.9 = (bf16[64,768]{1,0:T(8,128)(2,1)S(1)}, bf16[64,768]{1,0:T(8,128)(2,1)S(1)}, u32[]{:S(2)}, u32[]{:S(2)}) collective-permute-start(bf16[64,768]{1,0:T(8,128)(2,1)S(1)} %get-tuple-element.39), channel_id=1, source_target_pairs={{0,2},{2,0},{4,6},{6,4},{8,10},{10,8},{12,14},{14,12},{1,3},{3,1},... | collective-permute-start | bytes 294920 | tf_op jit(solution)/shard_map/ppermute | solution.py:248

commit v3 on v1

--- a/solution.py
+++ b/solution.py
@@ -248,21 +248,20 @@
     return lax.ppermute(value, axis, [(i, i ^ offset) for i in range(lax.axis_size(axis))])
 
 
-def step_from(k, owners):
-    return 0 if k == owners - 1 else k & (k - 1)
+GROUPS = (('own', (0,)), ('near', (1, 2, 4)), ('far', (5, 6)), ('last', (3, 7)))
+APART = ('own', 'near')
+ROWS = {4: 0, 2: 0, 1: 0, 7: 0, 6: 4, 5: 4, 3: 2}
+BACK = {7: 0, 6: 4, 5: 4, 3: 2, 4: 0, 2: 0, 1: 0}
 
 
 def routed_all(stream, whole, mine, weights, experts):
-    owners = lax.axis_size("ep")
     tokens = whole.shape[0]
-    near = [k for k in range(1, owners) if k & (k - 1) == 0]
-    far = [k for k in range(1, owners) if k not in near]
+    cols = stream.shape[1]
     half = {0: mine}
-    for k in sorted(near, reverse=True) + sorted(far, key=lambda k: (k.bit_count(), -k)):
-        source = step_from(k, owners)
+    for k, source in ROWS.items():
         half[k] = flip(half[source], "ep", k ^ source)
     total = {}
-    for name, group in (("own", [0]), ("near", near), ("far", far)):
+    for name, group in GROUPS:
         sources = [whole]
         if name != "own":
             sources = []
@@ -270,14 +269,17 @@
                 sources += [half[k], flip(half[k], "tp", 1)]
         kept, sent = expert(sources, *weights, experts)
         received = flip(sent, "tp", 1)
+        sums = []
         for i, k in enumerate(group):
             rows = slice(i * tokens, (i + 1) * tokens)
-            total[k] = kept[rows] + received[rows].astype(jnp.float32)
-    for k in sorted(range(1, owners), key=lambda k: (-k.bit_count(), -k)):
-        target = step_from(k, owners)
+            sums.append(kept[rows] + received[rows].astype(jnp.float32))
+        if name in APART:
+            sums = lax.optimization_barrier(tuple(sums))
+        total.update(zip(group, sums))
+    for k, target in BACK.items():
         part = flip(total[k].astype(jnp.bfloat16), "ep", k ^ target)
         total[target] = total[target] + part.astype(jnp.float32)
-    return (stream + total[0][:, : stream.shape[1]]).astype(jnp.bfloat16)
+    return (stream + total[0][:, :cols]).astype(jnp.bfloat16)
 
 
 def routed_slots(stream, normed, experts_chosen, router_logits, w_gate, w_up, w_down, capacity):

time: 58.2 us -> 57 us (0.979)
  waiting for transfers between devices: 24.4 us -> 20.9 us
  starting transfers between devices: 20.5 us -> 22.4 us
    ppermute x25 -> x26, waiting for transfers between devices: 24.4 us -> 20.9 us  [flip(): lax.ppermute(value, axis, [(i, i ^ offset) for i in range(lax.axis_size(a...]
    ppermute x25 -> x26, starting transfers between devices: 20.5 us -> 22.4 us  [flip(): lax.ppermute(value, axis, [(i, i ^ offset) for i in range(lax.axis_size(a...]
    pallas_call x3 -> x4, Pallas kernels: 5.57 us -> 6.01 us  [expert(): pl.pallas_call(functools.partial(expert_kernel, experts, pieces), out_sha...]
  transfers between devices with their start and end apart: 25 -> 26, of which waited for: 13 -> 10; matrix products, arithmetic and copies ran while one was open for 0% -> 0% of each run, Pallas kernels for 6% -> 11%
where the time goes in v3:
time: 57 us; the launch traced here: 56.8 us
  starting transfers between devices  22.4 us (39%)
  waiting for transfers between devices  20.9 us (37%)
  Pallas kernels  12.5 us (22%)
  other arithmetic  0.92 us (2%)
    ppermute x26, starting transfers between devices, flip(): lax.ppermute(value, axis, [(i, i ^ offset) for i in range(lax.axis_size(a...  22.4 us
    ppermute x26, waiting for transfers between devices, flip(): lax.ppermute(value, axis, [(i, i ^ offset) for i in range(lax.axis_size(a...  20.9 us
    pallas_call x1, Pallas kernels, attend(): pl.pallas_call(functools.partial(attend_kernel, heads, experts), out_shap...  6.22 us
    pallas_call x4, Pallas kernels, expert(): pl.pallas_call(functools.partial(expert_kernel, experts, pieces), out_sha...  6.01 us
  transfers between devices with their start and end apart: 26, of which 10 were waited for; matrix products, arithmetic and copies ran while one was open for 0% of the time, Pallas kernels for 11%

profile of v3, /device:TPU:0, one launch (start us, length us, event | category | flops | bytes accessed | tf_op | source)
XLA Modules:
  0.0 56.8 jit_solution(4650706627157042961)
XLA Ops:
  0.0 6.2 %attend.1 = (f32[64,1440]{1,0:T(8,128)S(1)}, bf16[64,1440]{1,0:T(8,128)(2,1)S(1)}, bf16[64,16]{1,0:T(8,128)(2,1)S(1)}, bf16[1440,720]{1,0:T(8,128)(2,1)S(1)}, bf...) custom-call(s32[12,64]{1,0:T(8,128)} %bitcast.11, s32[64]{0:T(128)} %length_in.1, bf16[64,1024]{1,0:T(8,128)(2,1)} %q_in.1, ...), custom_call_target="tpu_custom_call" | custom-call | tf_op jit(solution)/shard_map/attend/pallas_call | solution.py:136
  6.2 0.6 collective-permute-start
  6.8 1.1 %collective-permute-done.other = bf16[64,1440]{1,0:T(8,128)(2,1)S(1)} collective-permute-done((bf16[64,1440]{1,0:T(8,128)(2,1)S(1)}, bf16[64,1440]{1,0:T(8,128)(2,1)S(1)}, u32[]{:S(2)}, u32[]{:S(2)}) %collective-permute-start) | collective-permute-done | bytes 184352 | tf_op jit(solution)/shard_map/ppermute | solution.py:248
  7.9 0.2 norm.1
  8.1 2.9 %collective-permute-start.9 = (bf16[32,1536]{1,0:T(8,128)(2,1)S(1)}, bf16[32,1536]{1,0:T(8,128)(2,1)S(1)}, u32[]{:S(2)}, u32[]{:S(2)}) collective-permute-start(bf16[32,1536]{1,0:T(8,128)(2,1)S(1)} %get-tuple-element.35), channel_id=1, source_target_pairs={{0,2},{2,0},{4,6},{6,4},{8,10},{10,8},{12,14},{14,12},{1,3},{3,1},... | collective-permute-start | bytes 294920 | tf_op jit(solution)/shard_map/ppermute | solution.py:248
  11.0 1.6 %collective-permute-start.2 = (bf16[32,1536]{1,0:T(8,128)(2,1)S(1)}, bf16[32,1536]{1,0:T(8,128)(2,1)S(1)}, u32[]{:S(2)}, u32[]{:S(2)}) collective-permute-start(bf16[32,1536]{1,0:T(8,128)(2,1)S(1)} %get-tuple-element.35), channel_id=1, source_target_pairs={{0,4},{2,6},{4,0},{6,2},{8,12},{10,14},{12,8},{14,10},{1,5},{3,7},... | collective-permute-start | bytes 294920 | tf_op jit(solution)/shard_map/ppermute | solution.py:248
  12.6 2.6 %collective-permute-start.12 = (bf16[32,1536]{1,0:T(8,128)(2,1)S(1)}, bf16[32,1536]{1,0:T(8,128)(2,1)S(1)}, u32[]{:S(2)}, u32[]{:S(2)}) collective-permute-start(bf16[32,1536]{1,0:T(8,128)(2,1)S(1)} %get-tuple-element.35), channel_id=1, source_target_pairs={{0,8},{2,10},{4,12},{6,14},{8,0},{10,2},{12,4},{14,6},{1,9},{3,11}... | collective-permute-start | bytes 294920 | tf_op jit(solution)/shard_map/ppermute | solution.py:248
  15.2 0.4 collective-permute-done.2.refs_2_
  15.6 0.1 collective-permute-start.11
  15.7 4.2 %collective-permute-done.12.refs_4_ = bf16[32,1536]{1,0:T(8,128)(2,1)S(1)} collective-permute-done((bf16[32,1536]{1,0:T(8,128)(2,1)S(1)}, bf16[32,1536]{1,0:T(8,128)(2,1)S(1)}, u32[]{:S(2)}, u32[]{:S(2)}) %collective-permute-start.12) | collective-permute-done | bytes 98336 | tf_op jit(solution)/shard_map/ppermute | solution.py:248
  19.9 0.0 collective-permute-start.13
  19.9 2.4 %collective-permute-start.5 = (bf16[32,1536]{1,0:T(8,128)(2,1)S(1)}, bf16[32,1536]{1,0:T(8,128)(2,1)S(1)}, u32[]{:S(2)}, u32[]{:S(2)}) collective-permute-start(bf16[32,1536]{1,0:T(8,128)(2,1)S(1)} %get-tuple-element.35), channel_id=1, source_target_pairs={{0,14},{2,12},{4,10},{6,8},{8,6},{10,4},{12,2},{14,0},{1,15},{3,13... | collective-permute-start | bytes 294920 | tf_op jit(solution)/shard_map/ppermute | solution.py:248
  22.3 1.5 %collective-permute-start.3 = (bf16[32,1536]{1,0:T(8,128)(2,1)S(1)}, bf16[32,1536]{1,0:T(8,128)(2,1)S(1)}, u32[]{:S(2)}, u32[]{:S(2)}) collective-permute-start(bf16[32,1536]{1,0:T(8,128)(2,1)S(1)} %collective-permute-done.2.refs_2_), channel_id=1, source_target_pairs={{0,2},{2,0},{4,6},{6,4},{8,10},{10,8},{12,14},{14,12},{1,3},{3,1},... | collective-permute-start | bytes 294920 | tf_op jit(solution)/shard_map/ppermute | solution.py:248
  23.8 0.0 collective-permute-done.10.refs_1_
  23.8 0.0 collective-permute-done.11.refs_3_
  23.8 1.8 %expert.6 = (f32[192,768]{1,0:T(8,128)S(1)}, bf16[192,768]{1,0:T(8,128)(2,1)S(1)}) custom-call(bf16[32,1536]{1,0:T(8,128)(2,1)S(1)} %collective-permute-done.9.refs_0_, bf16[32,1536]{1,0:T(8,128)(2,1)S(1)} %collective-permute-done.10.refs_1_, bf16[32,1536]{1,0:T(8,128)(2,1)S(1)} %collective-permute-done.2.refs_2_, ...), custom_call_target="tpu_custom_call" | custom-call | flops 1194393600 | bytes 6220800 | tf_op jit(solution)/shard_map/expert/pallas_call | solution.py:230
  25.7 0.1 collective-permute-start.14
  25.8 0.6 %collective-permute-start.15 = (bf16[32,1536]{1,0:T(8,128)(2,1)S(1)}, bf16[32,1536]{1,0:T(8,128)(2,1)S(1)}, u32[]{:S(2)}, u32[]{:S(2)}) collective-permute-start(bf16[32,1536]{1,0:T(8,128)(2,1)S(1)} %collective-permute-done.12.refs_4_), channel_id=1, source_target_pairs={{0,2},{2,0},{4,6},{6,4},{8,10},{10,8},{12,14},{14,12},{1,3},{3,1},... | collective-permute-start | bytes 294920 | tf_op jit(solution)/shard_map/ppermute | solution.py:248
  26.4 1.6 %collective-permute-done.5.refs_2_ = bf16[32,1536]{1,0:T(8,128)(2,1)S(1)} collective-permute-done((bf16[32,1536]{1,0:T(8,128)(2,1)S(1)}, bf16[32,1536]{1,0:T(8,128)(2,1)S(1)}, u32[]{:S(2)}, u32[]{:S(2)}) %collective-permute-start.5) | collective-permute-done | bytes 98336 | tf_op jit(solution)/shard_map/ppermute | solution.py:248
  27.9 1.9 %collective-permute-done.3.refs_0_ = bf16[32,1536]{1,0:T(8,128)(2,1)S(1)} collective-permute-done((bf16[32,1536]{1,0:T(8,128)(2,1)S(1)}, bf16[32,1536]{1,0:T(8,128)(2,1)S(1)}, u32[]{:S(2)}, u32[]{:S(2)}) %collective-permute-start.3) | collective-permute-done | bytes 98336 | tf_op jit(solution)/shard_map/ppermute | solution.py:248
  29.9 1.6 %collective-permute-done.15.refs_0_ = bf16[32,1536]{1,0:T(8,128)(2,1)S(1)} collective-permute-done((bf16[32,1536]{1,0:T(8,128)(2,1)S(1)}, bf16[32,1536]{1,0:T(8,128)(2,1)S(1)}, u32[]{:S(2)}, u32[]{:S(2)}) %collective-permute-start.15) | collective-permute-done | bytes 98336 | tf_op jit(solution)/shard_map/ppermute | solution.py:248
  31.5 0.0 collective-permute-start.16
  31.5 0.0 collective-permute-done.17.refs_2_
  31.5 0.5 collective-permute-start.18
  32.0 1.4 %expert.4 = (f32[64,768]{1,0:T(8,128)S(1)}, bf16[64,768]{1,0:T(8,128)(2,1)S(1)}) custom-call(bf16[64,1536]{1,0:T(8,128)(2,1)S(1)} %get-tuple-element.29.refs_0_, bf16[1440,720]{1,0:T(8,128)(2,1)S(1)} %get-tuple-element.30.refs_1_.refs_4_.refs_6_, bf16[1440,720]{1,0:T(8,128)(2,1)S(1)} %get-tuple-element.31.refs_2_.refs_5_.refs_7_, ...), custom_call_target="tpu_custom_call" | custom-call | flops 398131200 | bytes 6220800 | tf_op jit(solution)/shard_map/expert/pallas_call | solution.py:230
  33.4 0.1 collective-permute-start.1
  33.5 0.0 collective-permute-done.4.refs_1_
  33.5 1.4 %expert.5 = (f32[128,768]{1,0:T(8,128)S(1)}, bf16[128,768]{1,0:T(8,128)(2,1)S(1)}) custom-call(bf16[32,1536]{1,0:T(8,128)(2,1)S(1)} %collective-permute-done.3.refs_0_, bf16[32,1536]{1,0:T(8,128)(2,1)S(1)} %collective-permute-done.4.refs_1_, bf16[32,1536]{1,0:T(8,128)(2,1)S(1)} %collective-permute-done.5.refs_2_, ...), custom_call_target="tpu_custom_call" | custom-call | flops 796262400 | bytes 6220800 | tf_op jit(solution)/shard_map/expert/pallas_call | solution.py:230
  34.9 0.6 collective-permute-start.7
  35.5 0.0 collective-permute-done.16.refs_1_
  35.5 0.0 collective-permute-done.18.refs_3_
  35.5 1.4 %expert.7 = (f32[128,768]{1,0:T(8,128)S(1)}, bf16[128,768]{1,0:T(8,128)(2,1)S(1)}) custom-call(bf16[32,1536]{1,0:T(8,128)(2,1)S(1)} %collective-permute-done.15.refs_0_, bf16[32,1536]{1,0:T(8,128)(2,1)S(1)} %collective-permute-done.16.refs_1_, bf16[32,1536]{1,0:T(8,128)(2,1)S(1)} %collective-permute-done.17.refs_2_, ...), custom_call_target="tpu_custom_call" | custom-call | flops 796262400 | bytes 6220800 | tf_op jit(solution)/shard_map/expert/pallas_call | solution.py:230
  36.8 0.1 collective-permute-start.19
  36.9 0.0 collective-permute-done.14
  37.0 1.3 %collective-permute-start.25 = (bf16[64,768]{1,0:T(8,128)(2,1)S(1)}, bf16[64,768]{1,0:T(8,128)(2,1)S(1)}, u32[]{:S(2)}, u32[]{:S(2)}) collective-permute-start(bf16[64,768]{1,0:T(8,128)(2,1)S(1)} %convert_add_fusion.2), channel_id=1, source_target_pairs={{0,2},{2,0},{4,6},{6,4},{8,10},{10,8},{12,14},{14,12},{1,3},{3,1},... | collective-permute-start | bytes 294920 | tf_op jit(solution)/shard_map/ppermute | solution.py:248
  38.3 0.0 collective-permute-done.7
  38.3 0.9 %collective-permute-start.23 = (bf16[64,768]{1,0:T(8,128)(2,1)S(1)}, bf16[64,768]{1,0:T(8,128)(2,1)S(1)}, u32[]{:S(2)}, u32[]{:S(2)}) collective-permute-start(bf16[64,768]{1,0:T(8,128)(2,1)S(1)} %get-tuple-element.48), channel_id=1, source_target_pairs={{0,2},{2,0},{4,6},{6,4},{8,10},{10,8},{12,14},{14,12},{1,3},{3,1},... | collective-permute-start | bytes 294920 | tf_op jit(solution)/shard_map/ppermute | solution.py:248
  39.2 0.0 collective-permute-done.19
  39.3 1.3 %collective-permute-start.21 = (bf16[64,768]{1,0:T(8,128)(2,1)S(1)}, bf16[64,768]{1,0:T(8,128)(2,1)S(1)}, u32[]{:S(2)}, u32[]{:S(2)}) collective-permute-start(bf16[64,768]{1,0:T(8,128)(2,1)S(1)} %get-tuple-element.50), channel_id=1, source_target_pairs={{0,2},{2,0},{4,6},{6,4},{8,10},{10,8},{12,14},{14,12},{1,3},{3,1},... | collective-permute-start | bytes 294920 | tf_op jit(solution)/shard_map/ppermute | solution.py:248
  40.5 0.3 collective-permute-start.20
  40.8 4.0 %collective-permute-done.23 = bf16[64,768]{1,0:T(8,128)(2,1)S(1)} collective-permute-done((bf16[64,768]{1,0:T(8,128)(2,1)S(1)}, bf16[64,768]{1,0:T(8,128)(2,1)S(1)}, u32[]{:S(2)}, u32[]{:S(2)}) %collective-permute-start.23) | collective-permute-done | bytes 98336 | tf_op jit(solution)/shard_map/ppermute | solution.py:248
  44.8 2.3 %collective-permute-start.8 = (bf16[64,768]{1,0:T(8,128)(2,1)S(1)}, bf16[64,768]{1,0:T(8,128)(2,1)S(1)}, u32[]{:S(2)}, u32[]{:S(2)}) collective-permute-start(bf16[64,768]{1,0:T(8,128)(2,1)S(1)} %get-tuple-element.47), channel_id=1, source_target_pairs={{0,14},{2,12},{4,10},{6,8},{8,6},{10,4},{12,2},{14,0},{1,15},{3,13... | collective-permute-start | bytes 294920 | tf_op jit(solution)/shard_map/ppermute | solution.py:248
  47.2 0.1 collective-permute-start.24
  47.3 2.8 %collective-permute-start.22 = (bf16[64,768]{1,0:T(8,128)(2,1)S(1)}, bf16[64,768]{1,0:T(8,128)(2,1)S(1)}, u32[]{:S(2)}, u32[]{:S(2)}) collective-permute-start(bf16[64,768]{1,0:T(8,128)(2,1)S(1)} %add_convert_fusion.2), channel_id=1, source_target_pairs={{0,8},{2,10},{4,12},{6,14},{8,0},{10,2},{12,4},{14,6},{1,9},{3,11}... | collective-permute-start | bytes 294920 | tf_op jit(solution)/shard_map/ppermute | solution.py:248
  50.1 3.2 %collective-permute-done.8 = bf16[64,768]{1,0:T(8,128)(2,1)S(1)} collective-permute-done((bf16[64,768]{1,0:T(8,128)(2,1)S(1)}, bf16[64,768]{1,0:T(8,128)(2,1)S(1)}, u32[]{:S(2)}, u32[]{:S(2)}) %collective-permute-start.8) | collective-permute-done | bytes 98336 | tf_op jit(solution)/shard_map/ppermute | solution.py:248
  53.3 0.3 collective-permute-done.24
  53.6 2.5 %collective-permute-done.22 = bf16[64,768]{1,0:T(8,128)(2,1)S(1)} collective-permute-done((bf16[64,768]{1,0:T(8,128)(2,1)S(1)}, bf16[64,768]{1,0:T(8,128)(2,1)S(1)}, u32[]{:S(2)}, u32[]{:S(2)}) %collective-permute-start.22) | collective-permute-done | bytes 98336 | tf_op jit(solution)/shard_map/ppermute | solution.py:248
  56.1 0.7 %fusion.4 = bf16[64,720]{1,0:T(8,128)(2,1)} fusion(f32[64,720]{1,0:T(8,128)S(1)} %get-tuple-element.28, f32[64,768]{1,0:T(8,128)S(1)} %convert_add_fusion.3, bf16[64,768]{1,0:T(8,128)(2,1)S(1)} %collective-permute-done.25, bf16[64,768]{1,0:T(8,128)(2,1)S(1)} %collective-permute-done.24, bf16[64,768]{1,0:T(8,128)(2,1)S(1)} %collective-permute-done.22, ...), kind=kLoop, calls=%fused_computation.5 | loop fusion | flops 460800 | bytes 829440 | tf_op jit(solution)/shard_map/convert_element_type | solution.py:282
  (23 shorter events, 0.2 us)
Async XLA Ops:
  0.0 6.8 %copy-start.1 = (f32[1440]{0:T(1024)S(1)}, f32[1440]{0:T(1024)}, u32[]{:S(2)}) copy-start(f32[1440]{0:T(1024)} %param.19) | copy-start | bytes 17284
  0.0 7.9 %copy-start = (bf16[64,1440]{1,0:T(8,128)(2,1)S(1)}, bf16[64,1440]{1,0:T(8,128)(2,1)}, u32[]{:S(2)}) copy-start(bf16[64,1440]{1,0:T(8,128)(2,1)} %resid.1) | copy-start | bytes 552964
  6.2 1.6 %collective-permute-start = (bf16[64,1440]{1,0:T(8,128)(2,1)S(1)}, bf16[64,1440]{1,0:T(8,128)(2,1)S(1)}, u32[]{:S(2)}, u32[]{:S(2)}) collective-permute-start(bf16[64,1440]{1,0:T(8,128)(2,1)S(1)} %get-tuple-element.26), channel_id=1, source_target_pairs={{0,1},{1,0},{2,3},{3,2},{4,5},{5,4},{6,7},{7,6},{8,9},{9,8},{10,11... | collective-permute-start | bytes 552968 | tf_op jit(solution)/shard_map/ppermute | solution.py:248
  8.1 7.1 %collective-permute-start.9 = (bf16[32,1536]{1,0:T(8,128)(2,1)S(1)}, bf16[32,1536]{1,0:T(8,128)(2,1)S(1)}, u32[]{:S(2)}, u32[]{:S(2)}) collective-permute-start(bf16[32,1536]{1,0:T(8,128)(2,1)S(1)} %get-tuple-element.35), channel_id=1, source_target_pairs={{0,2},{2,0},{4,6},{6,4},{8,10},{10,8},{12,14},{14,12},{1,3},{3,1},... | collective-permute-start | bytes 294920 | tf_op jit(solution)/shard_map/ppermute | solution.py:248
  11.0 4.6 %collective-permute-start.2 = (bf16[32,1536]{1,0:T(8,128)(2,1)S(1)}, bf16[32,1536]{1,0:T(8,128)(2,1)S(1)}, u32[]{:S(2)}, u32[]{:S(2)}) collective-permute-start(bf16[32,1536]{1,0:T(8,128)(2,1)S(1)} %get-tuple-element.35), channel_id=1, source_target_pairs={{0,4},{2,6},{4,0},{6,2},{8,12},{10,14},{12,8},{14,10},{1,5},{3,7},... | collective-permute-start | bytes 294920 | tf_op jit(solution)/shard_map/ppermute | solution.py:248
  12.6 7.3 %collective-permute-start.12 = (bf16[32,1536]{1,0:T(8,128)(2,1)S(1)}, bf16[32,1536]{1,0:T(8,128)(2,1)S(1)}, u32[]{:S(2)}, u32[]{:S(2)}) collective-permute-start(bf16[32,1536]{1,0:T(8,128)(2,1)S(1)} %get-tuple-element.35), channel_id=1, source_target_pairs={{0,8},{2,10},{4,12},{6,14},{8,0},{10,2},{12,4},{14,6},{1,9},{3,11}... | collective-permute-start | bytes 294920 | tf_op jit(solution)/shard_map/ppermute | solution.py:248
  15.2 8.6 %collective-permute-start.10 = (bf16[32,1536]{1,0:T(8,128)(2,1)S(1)}, bf16[32,1536]{1,0:T(8,128)(2,1)S(1)}, u32[]{:S(2)}, u32[]{:S(2)}) collective-permute-start(bf16[32,1536]{1,0:T(8,128)(2,1)S(1)} %collective-permute-done.9.refs_0_), channel_id=1, source_target_pairs={{0,1},{1,0},{2,3},{3,2},{4,5},{5,4},{6,7},{7,6},{8,9},{9,8},{10,11... | collective-permute-start | bytes 294920 | tf_op jit(solution)/shard_map/ppermute | solution.py:248
  15.6 8.2 %collective-permute-start.11 = (bf16[32,1536]{1,0:T(8,128)(2,1)S(1)}, bf16[32,1536]{1,0:T(8,128)(2,1)S(1)}, u32[]{:S(2)}, u32[]{:S(2)}) collective-permute-start(bf16[32,1536]{1,0:T(8,128)(2,1)S(1)} %collective-permute-done.2.refs_2_), channel_id=1, source_target_pairs={{0,1},{1,0},{2,3},{3,2},{4,5},{5,4},{6,7},{7,6},{8,9},{9,8},{10,11... | collective-permute-start | bytes 294920 | tf_op jit(solution)/shard_map/ppermute | solution.py:248
  19.9 3.9 %collective-permute-start.13 = (bf16[32,1536]{1,0:T(8,128)(2,1)S(1)}, bf16[32,1536]{1,0:T(8,128)(2,1)S(1)}, u32[]{:S(2)}, u32[]{:S(2)}) collective-permute-start(bf16[32,1536]{1,0:T(8,128)(2,1)S(1)} %collective-permute-done.12.refs_4_), channel_id=1, source_target_pairs={{0,1},{1,0},{2,3},{3,2},{4,5},{5,4},{6,7},{7,6},{8,9},{9,8},{10,11... | collective-permute-start | bytes 294920 | tf_op jit(solution)/shard_map/ppermute | solution.py:248
  19.9 8.0 %collective-permute-start.5 = (bf16[32,1536]{1,0:T(8,128)(2,1)S(1)}, bf16[32,1536]{1,0:T(8,128)(2,1)S(1)}, u32[]{:S(2)}, u32[]{:S(2)}) collective-permute-start(bf16[32,1536]{1,0:T(8,128)(2,1)S(1)} %get-tuple-element.35), channel_id=1, source_target_pairs={{0,14},{2,12},{4,10},{6,8},{8,6},{10,4},{12,2},{14,0},{1,15},{3,13... | collective-permute-start | bytes 294920 | tf_op jit(solution)/shard_map/ppermute | solution.py:248
  22.3 7.5 %collective-permute-start.3 = (bf16[32,1536]{1,0:T(8,128)(2,1)S(1)}, bf16[32,1536]{1,0:T(8,128)(2,1)S(1)}, u32[]{:S(2)}, u32[]{:S(2)}) collective-permute-start(bf16[32,1536]{1,0:T(8,128)(2,1)S(1)} %collective-permute-done.2.refs_2_), channel_id=1, source_target_pairs={{0,2},{2,0},{4,6},{6,4},{8,10},{10,8},{12,14},{14,12},{1,3},{3,1},... | collective-permute-start | bytes 294920 | tf_op jit(solution)/shard_map/ppermute | solution.py:248
  25.7 11.3 %collective-permute-start.14 = (bf16[192,768]{1,0:T(8,128)(2,1)S(1)}, bf16[192,768]{1,0:T(8,128)(2,1)S(1)}, u32[]{:S(2)}, u32[]{:S(2)}) collective-permute-start(bf16[192,768]{1,0:T(8,128)(2,1)S(1)} %get-tuple-element.39), channel_id=1, source_target_pairs={{0,1},{1,0},{2,3},{3,2},{4,5},{5,4},{6,7},{7,6},{8,9},{9,8},{10,11... | collective-permute-start | bytes 884744 | tf_op jit(solution)/shard_map/ppermute | solution.py:248
  25.8 5.7 %collective-permute-start.15 = (bf16[32,1536]{1,0:T(8,128)(2,1)S(1)}, bf16[32,1536]{1,0:T(8,128)(2,1)S(1)}, u32[]{:S(2)}, u32[]{:S(2)}) collective-permute-start(bf16[32,1536]{1,0:T(8,128)(2,1)S(1)} %collective-permute-done.12.refs_4_), channel_id=1, source_target_pairs={{0,2},{2,0},{4,6},{6,4},{8,10},{10,8},{12,14},{14,12},{1,3},{3,1},... | collective-permute-start | bytes 294920 | tf_op jit(solution)/shard_map/ppermute | solution.py:248
  26.3 5.1 %collective-permute-start.17 = (bf16[32,1536]{1,0:T(8,128)(2,1)S(1)}, bf16[32,1536]{1,0:T(8,128)(2,1)S(1)}, u32[]{:S(2)}, u32[]{:S(2)}) collective-permute-start(bf16[32,1536]{1,0:T(8,128)(2,1)S(1)} %collective-permute-done.12.refs_4_), channel_id=1, source_target_pairs={{0,4},{2,6},{4,0},{6,2},{8,12},{10,14},{12,8},{14,10},{1,5},{3,7},... | collective-permute-start | bytes 294920 | tf_op jit(solution)/shard_map/ppermute | solution.py:248
  27.9 5.5 %collective-permute-start.6 = (bf16[32,1536]{1,0:T(8,128)(2,1)S(1)}, bf16[32,1536]{1,0:T(8,128)(2,1)S(1)}, u32[]{:S(2)}, u32[]{:S(2)}) collective-permute-start(bf16[32,1536]{1,0:T(8,128)(2,1)S(1)} %collective-permute-done.5.refs_2_), channel_id=1, source_target_pairs={{0,1},{1,0},{2,3},{3,2},{4,5},{5,4},{6,7},{7,6},{8,9},{9,8},{10,11... | collective-permute-start | bytes 294920 | tf_op jit(solution)/shard_map/ppermute | solution.py:248
  29.9 3.6 %collective-permute-start.4 = (bf16[32,1536]{1,0:T(8,128)(2,1)S(1)}, bf16[32,1536]{1,0:T(8,128)(2,1)S(1)}, u32[]{:S(2)}, u32[]{:S(2)}) collective-permute-start(bf16[32,1536]{1,0:T(8,128)(2,1)S(1)} %collective-permute-done.3.refs_0_), channel_id=1, source_target_pairs={{0,1},{1,0},{2,3},{3,2},{4,5},{5,4},{6,7},{7,6},{8,9},{9,8},{10,11... | collective-permute-start | bytes 294920 | tf_op jit(solution)/shard_map/ppermute | solution.py:248
  31.5 4.0 %collective-permute-start.16 = (bf16[32,1536]{1,0:T(8,128)(2,1)S(1)}, bf16[32,1536]{1,0:T(8,128)(2,1)S(1)}, u32[]{:S(2)}, u32[]{:S(2)}) collective-permute-start(bf16[32,1536]{1,0:T(8,128)(2,1)S(1)} %collective-permute-done.15.refs_0_), channel_id=1, source_target_pairs={{0,1},{1,0},{2,3},{3,2},{4,5},{5,4},{6,7},{7,6},{8,9},{9,8},{10,11... | collective-permute-start | bytes 294920 | tf_op jit(solution)/shard_map/ppermute | solution.py:248
  31.5 4.0 %collective-permute-start.18 = (bf16[32,1536]{1,0:T(8,128)(2,1)S(1)}, bf16[32,1536]{1,0:T(8,128)(2,1)S(1)}, u32[]{:S(2)}, u32[]{:S(2)}) collective-permute-start(bf16[32,1536]{1,0:T(8,128)(2,1)S(1)} %collective-permute-done.17.refs_2_), channel_id=1, source_target_pairs={{0,1},{1,0},{2,3},{3,2},{4,5},{5,4},{6,7},{7,6},{8,9},{9,8},{10,11... | collective-permute-start | bytes 294920 | tf_op jit(solution)/shard_map/ppermute | solution.py:248
  33.4 16.7 %collective-permute-start.1 = (bf16[64,768]{1,0:T(8,128)(2,1)S(1)}, bf16[64,768]{1,0:T(8,128)(2,1)S(1)}, u32[]{:S(2)}, u32[]{:S(2)}) collective-permute-start(bf16[64,768]{1,0:T(8,128)(2,1)S(1)} %get-tuple-element.34), channel_id=1, source_target_pairs={{0,1},{1,0},{2,3},{3,2},{4,5},{5,4},{6,7},{7,6},{8,9},{9,8},{10,11... | collective-permute-start | bytes 294920 | tf_op jit(solution)/shard_map/ppermute | solution.py:248
  34.9 3.4 %collective-permute-start.7 = (bf16[128,768]{1,0:T(8,128)(2,1)S(1)}, bf16[128,768]{1,0:T(8,128)(2,1)S(1)}, u32[]{:S(2)}, u32[]{:S(2)}) collective-permute-start(bf16[128,768]{1,0:T(8,128)(2,1)S(1)} %get-tuple-element.37), channel_id=1, source_target_pairs={{0,1},{1,0},{2,3},{3,2},{4,5},{5,4},{6,7},{7,6},{8,9},{9,8},{10,11... | collective-permute-start | bytes 589832 | tf_op jit(solution)/shard_map/ppermute | solution.py:248
  36.8 2.4 %collective-permute-start.19 = (bf16[128,768]{1,0:T(8,128)(2,1)S(1)}, bf16[128,768]{1,0:T(8,128)(2,1)S(1)}, u32[]{:S(2)}, u32[]{:S(2)}) collective-permute-start(bf16[128,768]{1,0:T(8,128)(2,1)S(1)} %get-tuple-element.42), channel_id=1, source_target_pairs={{0,1},{1,0},{2,3},{3,2},{4,5},{5,4},{6,7},{7,6},{8,9},{9,8},{10,11... | collective-permute-start | bytes 589832 | tf_op jit(solution)/shard_map/ppermute | solution.py:248
  37.0 13.1 %collective-permute-start.25 = (bf16[64,768]{1,0:T(8,128)(2,1)S(1)}, bf16[64,768]{1,0:T(8,128)(2,1)S(1)}, u32[]{:S(2)}, u32[]{:S(2)}) collective-permute-start(bf16[64,768]{1,0:T(8,128)(2,1)S(1)} %convert_add_fusion.2), channel_id=1, source_target_pairs={{0,2},{2,0},{4,6},{6,4},{8,10},{10,8},{12,14},{14,12},{1,3},{3,1},... | collective-permute-start | bytes 294920 | tf_op jit(solution)/shard_map/ppermute | solution.py:248
  38.3 6.5 %collective-permute-start.23 = (bf16[64,768]{1,0:T(8,128)(2,1)S(1)}, bf16[64,768]{1,0:T(8,128)(2,1)S(1)}, u32[]{:S(2)}, u32[]{:S(2)}) collective-permute-start(bf16[64,768]{1,0:T(8,128)(2,1)S(1)} %get-tuple-element.48), channel_id=1, source_target_pairs={{0,2},{2,0},{4,6},{6,4},{8,10},{10,8},{12,14},{14,12},{1,3},{3,1},... | collective-permute-start | bytes 294920 | tf_op jit(solution)/shard_map/ppermute | solution.py:248
  39.3 7.9 %collective-permute-start.21 = (bf16[64,768]{1,0:T(8,128)(2,1)S(1)}, bf16[64,768]{1,0:T(8,128)(2,1)S(1)}, u32[]{:S(2)}, u32[]{:S(2)}) collective-permute-start(bf16[64,768]{1,0:T(8,128)(2,1)S(1)} %get-tuple-element.50), channel_id=1, source_target_pairs={{0,2},{2,0},{4,6},{6,4},{8,10},{10,8},{12,14},{14,12},{1,3},{3,1},... | collective-permute-start | bytes 294920 | tf_op jit(solution)/shard_map/ppermute | solution.py:248
  40.5 6.7 %collective-permute-start.20 = (bf16[64,768]{1,0:T(8,128)(2,1)S(1)}, bf16[64,768]{1,0:T(8,128)(2,1)S(1)}, u32[]{:S(2)}, u32[]{:S(2)}) collective-permute-start(bf16[64,768]{1,0:T(8,128)(2,1)S(1)} %get-tuple-element.49), channel_id=1, source_target_pairs={{0,4},{2,6},{4,0},{6,2},{8,12},{10,14},{12,8},{14,10},{1,5},{3,7},... | collective-permute-start | bytes 294920 | tf_op jit(solution)/shard_map/ppermute | solution.py:248
  44.8 8.5 %collective-permute-start.8 = (bf16[64,768]{1,0:T(8,128)(2,1)S(1)}, bf16[64,768]{1,0:T(8,128)(2,1)S(1)}, u32[]{:S(2)}, u32[]{:S(2)}) collective-permute-start(bf16[64,768]{1,0:T(8,128)(2,1)S(1)} %get-tuple-element.47), channel_id=1, source_target_pairs={{0,14},{2,12},{4,10},{6,8},{8,6},{10,4},{12,2},{14,0},{1,15},{3,13... | collective-permute-start | bytes 294920 | tf_op jit(solution)/shard_map/ppermute | solution.py:248
  47.2 6.4 %collective-permute-start.24 = (bf16[64,768]{1,0:T(8,128)(2,1)S(1)}, bf16[64,768]{1,0:T(8,128)(2,1)S(1)}, u32[]{:S(2)}, u32[]{:S(2)}) collective-permute-start(bf16[64,768]{1,0:T(8,128)(2,1)S(1)} %add_convert_fusion), channel_id=1, source_target_pairs={{0,4},{2,6},{4,0},{6,2},{8,12},{10,14},{12,8},{14,10},{1,5},{3,7},... | collective-permute-start | bytes 294920 | tf_op jit(solution)/shard_map/ppermute | solution.py:248
  47.3 8.8 %collective-permute-start.22 = (bf16[64,768]{1,0:T(8,128)(2,1)S(1)}, bf16[64,768]{1,0:T(8,128)(2,1)S(1)}, u32[]{:S(2)}, u32[]{:S(2)}) collective-permute-start(bf16[64,768]{1,0:T(8,128)(2,1)S(1)} %add_convert_fusion.2), channel_id=1, source_target_pairs={{0,8},{2,10},{4,12},{6,14},{8,0},{10,2},{12,4},{14,6},{1,9},{3,11}... | collective-permute-start | bytes 294920 | tf_op jit(solution)/shard_map/ppermute | solution.py:248
